TPU v7x, 128 devices: a whole 4x4x4 slice. The times are simulated.
128 devices in a mesh: blk: 8 (over z, y_hi), slab: 16 (over x, y_lo, core).
Axes of the slice: x: 4, y: 4 (y_hi: 2, y_lo: 2; y = y_hi * 2 + y_lo), z: 4, core: 2. Of those that a mesh axis runs over, the one named last changes fastest.
Arguments:
- new_rows: bfloat16 [65536, 768], P(('blk', 'slab')), may hold values from -6 to 6
- index_rows: bfloat16 [32768, 768], P('blk'), may hold values from -6 to 6
- pattern: int32 [128, 8], replicated, may hold values from 0 to 1, as said below
- kept_row: int32 [32768], P(('blk', 'slab')), may hold values from 0 to 511
- kept_owner: int32 [32768, 1], P(('blk', 'slab')), may hold values from 0 to 127; in each aligned block of 256 rows (0 to 255, 256 to 511, ...) at most 4 rows name the same one
- kept_local: int32 [32768], P(('blk', 'slab')), may hold values from 0 to 15
Outputs:
- best_cosine: float32 [65536], P(('blk', 'slab'))
- centroid_sums: float32 [2048, 768], P(('blk', 'slab'))
- kept_counts: float32 [2048], P(('blk', 'slab'))
Inputs may be any that keep to these rules, and one draw needn't show every extreme that they name: `pattern`: every row has at least one 1. `kept_owner`: the 256 entries of one device name one owner at most 4 times, a bound that some block reaches.
All inputs are finite; a program needn't handle non-finite values.
Results may differ from a plain program's by a relative error of at most 0.0029.
Values may be sent and summed in bfloat16 or wider, within the bound.
A program may use at most 64 MiB of HBM per device.

v0:
```python
import jax
import jax.numpy as jnp
from jax import lax
from jax.sharding import PartitionSpec as P

CL_DEV = 16


EPS = 1e-06


def shifted(value, axis, steps):
    count = lax.axis_size(axis)
    pairs = [(source, (source + steps) % count) for source in range(count)]
    return lax.ppermute(value, axis, pairs)


def sent_together(arrays, axis, split_dim, concat_dim, along):
    both = jnp.concatenate(arrays, axis=along)
    out, at, done = (
        lax.all_to_all(both, axis, split_axis=split_dim, concat_axis=concat_dim, tiled=True),
        0,
        [],
    )
    for a in arrays:
        done.append(lax.slice_in_dim(out, at, at + a.shape[along], axis=along))
        at += a.shape[along]
    return tuple(done)


def unit_rows(values):
    wide = values.astype(jnp.float32)
    scale = lax.rsqrt(jnp.sum(wide * wide, axis=-1, keepdims=True) + EPS)
    return (wide * scale).astype(jnp.bfloat16)


def per_device(new_rows, index_rows, pattern, kept_row, kept_owner, kept_local):
    cycle = lax.axis_size("blk")
    lanes = lax.axis_size("slab")
    here = lax.axis_index("blk")
    lane = lax.axis_index("slab")
    new_unit = unit_rows(new_rows)
    index_unit = unit_rows(index_rows)

    def tile_max(rows, offset):
        anchor = (here - offset) % cycle
        active = pattern[anchor * lanes + lane, here] > 0
        scores = lax.dot_general(
            rows, index_unit, (((1,), (1,)), ((), ())), preferred_element_type=jnp.float32
        )
        return jnp.where(active, jnp.max(scores, axis=1), jnp.float32(-2.0))

    slots = {0: tile_max(new_unit, 0)}
    ahead_steps = cycle // 2
    moving = new_unit
    for step in range(1, ahead_steps + 1):
        moving = shifted(moving, "blk", 1)
        slots[step] = tile_max(moving, step)
    behind = new_unit
    for step in range(1, cycle - ahead_steps):
        behind = shifted(behind, "blk", -1)
        slots[cycle - step] = tile_max(behind, cycle - step)
    stacked = jnp.stack([slots[offset] for offset in range(cycle)], axis=0)
    order = (here - jnp.arange(cycle, dtype=jnp.int32)) % cycle
    by_anchor = jnp.take(stacked, order, axis=0)
    returned = lax.all_to_all(by_anchor, "blk", split_axis=0, concat_axis=0, tiled=True)
    best = jnp.max(returned, axis=0)
    picked = new_unit[kept_row]
    owner = kept_owner[:, 0]
    devices = cycle * lanes
    entries = kept_row.shape[0]
    local_tags = (kept_local[:, None] == jnp.arange(CL_DEV, dtype=jnp.int32)[None, :]).astype(
        jnp.bfloat16
    )
    capacity = (entries + devices - 1) // devices * 2
    position = jnp.arange(entries, dtype=jnp.int32)
    same_owner = owner[:, None] == owner[None, :]
    earlier = position[:, None] > position[None, :]
    rank = jnp.sum((same_owner & earlier).astype(jnp.int32), axis=1)
    target = owner * capacity + rank
    placing = (jnp.arange(devices * capacity, dtype=jnp.int32)[:, None] == target[None, :]).astype(
        jnp.bfloat16
    )
    payload = jnp.dot(placing, picked, preferred_element_type=jnp.float32).astype(jnp.bfloat16)
    tagging = jnp.dot(placing, local_tags, preferred_element_type=jnp.float32).astype(jnp.bfloat16)
    got_rows, got_tags = sent_together((payload, tagging), ("blk", "slab"), 0, 0, 1)
    sums = lax.dot_general(
        got_tags, got_rows, (((0,), (0,)), ((), ())), preferred_element_type=jnp.float32
    )
    counts = jnp.sum(got_tags.astype(jnp.float32), axis=0)
    return (best, sums, counts)


def solution(mesh):
    placed = (
        P(("blk", "slab"), None),
        P("blk", None),
        P(),
        P(("blk", "slab")),
        P(("blk", "slab"), None),
        P(("blk", "slab")),
    )
    return jax.shard_map(
        per_device,
        mesh=mesh,
        in_specs=placed,
        out_specs=(P(("blk", "slab")), P(("blk", "slab"), None), P(("blk", "slab"))),
        check_vma=False,
    )
```

profile of v0, /device:TPU:1, one launch (start us, length us, event | category | flops | bytes accessed | tf_op | source)
XLA Modules:
  0.0 158.8 jit_solution(8424456486347938531)
XLA Ops:
  0.6 1.4 fusion.2
  2.0 0.0 copy-start
  2.0 1.3 fusion.3
  3.3 7.3 %collective-permute-start.4 = (bf16[512,768]{1,0:T(8,128)(2,1)S(1)}, bf16[512,768]{1,0:T(8,128)(2,1)}, u32[]{:S(2)}, u32[]{:S(2)}) collective-permute-start(bf16[512,768]{1,0:T(8,128)(2,1)S(1)} %fusion.3), channel_id=1, source_target_pairs={{0,112},{16,0},{32,16},{48,32},{64,48},{80,64},{96,80},{112,96},{1... | collective-permute-start | bytes 2359304 | tf_op jit(solution)/shard_map/ppermute | solution.py:15
  10.6 0.0 collective-permute-start
  10.6 0.7 compare_select_fusion
  11.3 0.9 convert_reduce_fusion.1
  12.3 0.7 multiply_add_fusion
  12.9 0.9 convolution_convert_fusion.1
  13.9 0.1 copy.16
  14.0 1.2 gather_fusion.1
  15.2 0.4 convolution_convert_fusion
  15.6 0.1 pad_maximum_fusion
  15.7 1.2 all_to_all.13
  16.8 9.9 %all-to-all-start.1 = ((bf16[128,4,784]{2,1,0:T(4,128)(2,1)}), bf16[128,4,784]{2,1,0:T(4,128)(2,1)S(1)}, u32[]{:S(2)}, u32[]{:S(2)}) async-start(bf16[128,4,784]{2,1,0:T(4,128)(2,1)} %all_to_all.13), calls=%async_computation.1 | async-start | bytes 1835008 | tf_op jit(solution)/shard_map/all_to_all | solution.py:21
  27.0 0.0 copy-done
  27.0 0.7 fusion.22
  32.8 0.0 slice-start
  32.8 4.2 %fusion = f32[4096]{0:T(1024)S(1)} fusion(bf16[4096,768]{1,0:T(8,128)(2,1)} %param.7), kind=kLoop, calls=%fused_computation.4 | loop fusion | flops 9433088 | bytes 6307840 | tf_op jit(solution)/shard_map/reduce_sum | solution.py:33
  37.1 0.0 slice-start.1
  37.1 6.6 %convolution_reduce_fusion.7 = f32[512]{0:T(512)S(1)} fusion(bf16[512,768]{1,0:T(8,128)(2,1)S(1)} %fusion.3, bf16[4096,768]{1,0:T(8,128)(2,1)} %param.7, f32[4096]{0:T(1024)S(1)} %add_rsqrt_fusion), kind=kOutput, calls=%fused_computation.13 | convolution fusion | flops 3232759296 | bytes 7096320 | tf_op jit(solution)/shard_map/dot_general | solution.py:48
  43.7 0.0 collective-permute-done.4
  43.7 5.9 %collective-permute-start.5 = (bf16[512,768]{1,0:T(8,128)(2,1)}, bf16[512,768]{1,0:T(8,128)(2,1)}, u32[]{:S(2)}, u32[]{:S(2)}) collective-permute-start(bf16[512,768]{1,0:T(8,128)(2,1)} %collective-permute-done.4), channel_id=1, source_target_pairs={{0,112},{16,0},{32,16},{48,32},{64,48},{80,64},{96,80},{112,96},{1... | collective-permute-start | bytes 2359304 | tf_op jit(solution)/shard_map/ppermute | solution.py:15
  49.5 0.0 slice-done
  49.5 0.0 slice-done.1
  49.5 5.1 %convolution_reduce_fusion = f32[512]{0:T(512)S(1)} fusion(bf16[512,768]{1,0:T(8,128)(2,1)} %collective-permute-done.4, bf16[4096,768]{1,0:T(8,128)(2,1)S(1)} %bitcast.31, f32[4096]{0:T(1024)S(1)} %add_rsqrt_fusion), kind=kOutput, calls=%fused_computation.6 | convolution fusion | flops 3232759296 | bytes 7096320 | tf_op jit(solution)/shard_map/dot_general | solution.py:48
  54.7 0.0 collective-permute-done
  54.7 4.1 %convolution_reduce_fusion.6 = f32[512]{0:T(512)S(1)} fusion(bf16[512,768]{1,0:T(8,128)(2,1)S(1)} %collective-permute-done, bf16[4096,768]{1,0:T(8,128)(2,1)S(1)} %bitcast.31, f32[4096]{0:T(1024)S(1)} %add_rsqrt_fusion), kind=kOutput, calls=%fused_computation.12 | convolution fusion | flops 3232759296 | bytes 7096320 | tf_op jit(solution)/shard_map/dot_general | solution.py:48
  58.8 0.6 collective-permute-start.1
  59.4 0.0 all-to-all-done.1
  59.4 0.5 all_to_all.15
  59.8 0.0 slice-start.2
  59.8 0.9 fusion.4
  60.7 0.0 slice-start.3
  60.7 10.1 %collective-permute-done.5 = bf16[512,768]{1,0:T(8,128)(2,1)} collective-permute-done((bf16[512,768]{1,0:T(8,128)(2,1)}, bf16[512,768]{1,0:T(8,128)(2,1)}, u32[]{:S(2)}, u32[]{:S(2)}) %collective-permute-start.5) | collective-permute-done | bytes 786464 | tf_op jit(solution)/shard_map/ppermute | solution.py:15
  70.8 5.8 %collective-permute-start.6 = (bf16[512,768]{1,0:T(8,128)(2,1)}, bf16[512,768]{1,0:T(8,128)(2,1)S(1)}, u32[]{:S(2)}, u32[]{:S(2)}) collective-permute-start(bf16[512,768]{1,0:T(8,128)(2,1)} %collective-permute-done.5), channel_id=1, source_target_pairs={{0,112},{16,0},{32,16},{48,32},{64,48},{80,64},{96,80},{112,96},{1... | collective-permute-start | bytes 2359304 | tf_op jit(solution)/shard_map/ppermute | solution.py:15
  76.6 6.7 %convolution_reduce_fusion.1 = f32[512]{0:T(512)S(1)} fusion(bf16[512,768]{1,0:T(8,128)(2,1)} %collective-permute-done.5, bf16[4096,768]{1,0:T(8,128)(2,1)} %param.7, f32[4096]{0:T(1024)S(1)} %add_rsqrt_fusion), kind=kOutput, calls=%fused_computation.7 | convolution fusion | flops 3232759296 | bytes 7096320 | tf_op jit(solution)/shard_map/dot_general | solution.py:48
  83.3 5.1 %collective-permute-done.1 = bf16[512,768]{1,0:T(8,128)(2,1)} collective-permute-done((bf16[512,768]{1,0:T(8,128)(2,1)S(1)}, bf16[512,768]{1,0:T(8,128)(2,1)}, u32[]{:S(2)}, u32[]{:S(2)}) %collective-permute-start.1) | collective-permute-done | bytes 786464 | tf_op jit(solution)/shard_map/ppermute | solution.py:15
  88.3 3.0 %collective-permute-start.2 = (bf16[512,768]{1,0:T(8,128)(2,1)}, bf16[512,768]{1,0:T(8,128)(2,1)S(1)}, u32[]{:S(2)}, u32[]{:S(2)}) collective-permute-start(bf16[512,768]{1,0:T(8,128)(2,1)} %collective-permute-done.1), channel_id=1, source_target_pairs={{0,16},{16,32},{32,48},{48,64},{64,80},{80,96},{96,112},{112,0},{1... | collective-permute-start | bytes 2359304 | tf_op jit(solution)/shard_map/ppermute | solution.py:15
  91.3 0.0 slice-done.2
  91.3 0.0 slice-done.3
  91.3 5.1 %convolution_reduce_fusion.5 = f32[512]{0:T(512)S(1)} fusion(bf16[512,768]{1,0:T(8,128)(2,1)} %collective-permute-done.1, bf16[4096,768]{1,0:T(8,128)(2,1)S(1)} %bitcast.33, f32[4096]{0:T(1024)S(1)} %add_rsqrt_fusion), kind=kOutput, calls=%fused_computation.11 | convolution fusion | flops 3232759296 | bytes 7096320 | tf_op jit(solution)/shard_map/dot_general | solution.py:48
  96.5 8.0 %collective-permute-done.6 = bf16[512,768]{1,0:T(8,128)(2,1)S(1)} collective-permute-done((bf16[512,768]{1,0:T(8,128)(2,1)}, bf16[512,768]{1,0:T(8,128)(2,1)S(1)}, u32[]{:S(2)}, u32[]{:S(2)}) %collective-permute-start.6) | collective-permute-done | bytes 786464 | tf_op jit(solution)/shard_map/ppermute | solution.py:15
  104.5 4.0 %convolution_reduce_fusion.2 = f32[512]{0:T(512)S(1)} fusion(bf16[512,768]{1,0:T(8,128)(2,1)S(1)} %collective-permute-done.6, bf16[4096,768]{1,0:T(8,128)(2,1)S(1)} %bitcast.33, f32[4096]{0:T(1024)S(1)} %add_rsqrt_fusion), kind=kOutput, calls=%fused_computation.8 | convolution fusion | flops 3232759296 | bytes 7096320 | tf_op jit(solution)/shard_map/dot_general | solution.py:48
  108.5 13.5 %collective-permute-done.2 = bf16[512,768]{1,0:T(8,128)(2,1)S(1)} collective-permute-done((bf16[512,768]{1,0:T(8,128)(2,1)}, bf16[512,768]{1,0:T(8,128)(2,1)S(1)}, u32[]{:S(2)}, u32[]{:S(2)}) %collective-permute-start.2) | collective-permute-done | bytes 786464 | tf_op jit(solution)/shard_map/ppermute | solution.py:15
  122.0 3.0 %collective-permute-start.3 = (bf16[512,768]{1,0:T(8,128)(2,1)S(1)}, bf16[512,768]{1,0:T(8,128)(2,1)S(1)}, u32[]{:S(2)}, u32[]{:S(2)}) collective-permute-start(bf16[512,768]{1,0:T(8,128)(2,1)S(1)} %collective-permute-done.2), channel_id=1, source_target_pairs={{0,16},{16,32},{32,48},{48,64},{64,80},{80,96},{96,112},{112,0},{1... | collective-permute-start | bytes 2359304 | tf_op jit(solution)/shard_map/ppermute | solution.py:15
  124.9 4.0 %convolution_reduce_fusion.4 = f32[512]{0:T(512)S(1)} fusion(bf16[512,768]{1,0:T(8,128)(2,1)S(1)} %collective-permute-done.2, bf16[4096,768]{1,0:T(8,128)(2,1)S(1)} %bitcast.33, f32[4096]{0:T(1024)S(1)} %add_rsqrt_fusion), kind=kOutput, calls=%fused_computation.10 | convolution fusion | flops 3232759296 | bytes 7096320 | tf_op jit(solution)/shard_map/dot_general | solution.py:48
  128.9 14.1 %collective-permute-done.3 = bf16[512,768]{1,0:T(8,128)(2,1)S(1)} collective-permute-done((bf16[512,768]{1,0:T(8,128)(2,1)S(1)}, bf16[512,768]{1,0:T(8,128)(2,1)S(1)}, u32[]{:S(2)}, u32[]{:S(2)}) %collective-permute-start.3) | collective-permute-done | bytes 786464 | tf_op jit(solution)/shard_map/ppermute | solution.py:15
  143.1 4.0 %convolution_reduce_fusion.3 = f32[512]{0:T(512)S(1)} fusion(bf16[512,768]{1,0:T(8,128)(2,1)S(1)} %collective-permute-done.3, bf16[4096,768]{1,0:T(8,128)(2,1)S(1)} %bitcast.33, f32[4096]{0:T(1024)S(1)} %add_rsqrt_fusion), kind=kOutput, calls=%fused_computation.9 | convolution fusion | flops 3232759296 | bytes 7096320 | tf_op jit(solution)/shard_map/dot_general | solution.py:48
  147.1 0.6 gather_fusion
  147.7 0.1 bitcast_select_fusion
  147.7 0.6 copy.15
  148.3 3.3 %all-to-all-start = ((f32[8,1,512]{2,1,0:T(1,128)}), f32[8,1,512]{2,1,0:T(1,128)S(1)}, u32[]{:S(2)}, u32[]{:S(2)}) async-start(f32[8,1,512]{2,1,0:T(1,128)} %copy.15), calls=%async_computation | async-start | bytes 32768 | tf_op jit(solution)/shard_map/all_to_all | solution.py:66
  151.7 0.6 convert_reduce_fusion
  152.3 5.9 %all-to-all-done = f32[8,1,512]{2,1,0:T(1,128)S(1)} async-done(((f32[8,1,512]{2,1,0:T(1,128)}), f32[8,1,512]{2,1,0:T(1,128)S(1)}, u32[]{:S(2)}, u32[]{:S(2)}) %all-to-all-start) | async-done | bytes 16416 | tf_op jit(solution)/shard_map/all_to_all | solution.py:66
  158.2 0.6 reduce_max.89
  (17 shorter events, 0.1 us)
Async XLA Ops:
  2.0 25.0 %copy-start = (s32[128,8]{0,1:T(8,128)S(1)}, s32[128,8]{0,1:T(8,128)}, u32[]{:S(2)}) copy-start(s32[128,8]{0,1:T(8,128)} %param.8) | copy-start | bytes 12292
  3.3 40.3 %collective-permute-start.4 = (bf16[512,768]{1,0:T(8,128)(2,1)S(1)}, bf16[512,768]{1,0:T(8,128)(2,1)}, u32[]{:S(2)}, u32[]{:S(2)}) collective-permute-start(bf16[512,768]{1,0:T(8,128)(2,1)S(1)} %fusion.3), channel_id=1, source_target_pairs={{0,112},{16,0},{32,16},{48,32},{64,48},{80,64},{96,80},{112,96},{1... | collective-permute-start | bytes 2359304 | tf_op jit(solution)/shard_map/ppermute | solution.py:15
  10.6 44.1 %collective-permute-start = (bf16[512,768]{1,0:T(8,128)(2,1)S(1)}, bf16[512,768]{1,0:T(8,128)(2,1)S(1)}, u32[]{:S(2)}, u32[]{:S(2)}) collective-permute-start(bf16[512,768]{1,0:T(8,128)(2,1)S(1)} %fusion.3), channel_id=1, source_target_pairs={{0,16},{16,32},{32,48},{48,64},{64,80},{80,96},{96,112},{112,0},{1... | collective-permute-start | bytes 2359304 | tf_op jit(solution)/shard_map/ppermute | solution.py:15
  16.8 42.5 %all-to-all-start.1 = ((bf16[128,4,784]{2,1,0:T(4,128)(2,1)}), bf16[128,4,784]{2,1,0:T(4,128)(2,1)S(1)}, u32[]{:S(2)}, u32[]{:S(2)}) async-start(bf16[128,4,784]{2,1,0:T(4,128)(2,1)} %all_to_all.13), calls=%async_computation.1 | async-start | bytes 1835008 | tf_op jit(solution)/shard_map/all_to_all | solution.py:21
  32.8 16.7 %slice-start = ((s8[6291456]{0:T(1024)(128)(4,1)}), s8[4194304]{0:T(1024)(128)(4,1)S(1)}, s32[]{:S(2)}) async-start(s8[6291456]{0:T(1024)(128)(4,1)} %bitcast.30), calls=%async_computation.2 | async-start | bytes 8388608
  37.1 12.5 %slice-start.1 = ((s8[6291456]{0:T(1024)(128)(4,1)}), s8[2097152]{0:T(1024)(128)(4,1)S(1)}, s32[]{:S(2)}) async-start(s8[6291456]{0:T(1024)(128)(4,1)} %bitcast.30), calls=%async_computation.3 | async-start | bytes 4194304
  43.7 27.1 %collective-permute-start.5 = (bf16[512,768]{1,0:T(8,128)(2,1)}, bf16[512,768]{1,0:T(8,128)(2,1)}, u32[]{:S(2)}, u32[]{:S(2)}) collective-permute-start(bf16[512,768]{1,0:T(8,128)(2,1)} %collective-permute-done.4), channel_id=1, source_target_pairs={{0,112},{16,0},{32,16},{48,32},{64,48},{80,64},{96,80},{112,96},{1... | collective-permute-start | bytes 2359304 | tf_op jit(solution)/shard_map/ppermute | solution.py:15
  58.8 29.6 %collective-permute-start.1 = (bf16[512,768]{1,0:T(8,128)(2,1)S(1)}, bf16[512,768]{1,0:T(8,128)(2,1)}, u32[]{:S(2)}, u32[]{:S(2)}) collective-permute-start(bf16[512,768]{1,0:T(8,128)(2,1)S(1)} %collective-permute-done), channel_id=1, source_target_pairs={{0,16},{16,32},{32,48},{48,64},{64,80},{80,96},{96,112},{112,0},{1... | collective-permute-start | bytes 2359304 | tf_op jit(solution)/shard_map/ppermute | solution.py:15
  59.8 31.5 %slice-start.2 = ((s8[6291456]{0:T(1024)(128)(4,1)}), s8[4194304]{0:T(1024)(128)(4,1)S(1)}, s32[]{:S(2)}) async-start(s8[6291456]{0:T(1024)(128)(4,1)} %bitcast.32), calls=%async_computation.4 | async-start | bytes 8388608
  60.7 30.6 %slice-start.3 = ((s8[6291456]{0:T(1024)(128)(4,1)}), s8[2097152]{0:T(1024)(128)(4,1)S(1)}, s32[]{:S(2)}) async-start(s8[6291456]{0:T(1024)(128)(4,1)} %bitcast.32), calls=%async_computation.5 | async-start | bytes 4194304
  70.8 33.7 %collective-permute-start.6 = (bf16[512,768]{1,0:T(8,128)(2,1)}, bf16[512,768]{1,0:T(8,128)(2,1)S(1)}, u32[]{:S(2)}, u32[]{:S(2)}) collective-permute-start(bf16[512,768]{1,0:T(8,128)(2,1)} %collective-permute-done.5), channel_id=1, source_target_pairs={{0,112},{16,0},{32,16},{48,32},{64,48},{80,64},{96,80},{112,96},{1... | collective-permute-start | bytes 2359304 | tf_op jit(solution)/shard_map/ppermute | solution.py:15
  88.3 33.6 %collective-permute-start.2 = (bf16[512,768]{1,0:T(8,128)(2,1)}, bf16[512,768]{1,0:T(8,128)(2,1)S(1)}, u32[]{:S(2)}, u32[]{:S(2)}) collective-permute-start(bf16[512,768]{1,0:T(8,128)(2,1)} %collective-permute-done.1), channel_id=1, source_target_pairs={{0,16},{16,32},{32,48},{48,64},{64,80},{80,96},{96,112},{112,0},{1... | collective-permute-start | bytes 2359304 | tf_op jit(solution)/shard_map/ppermute | solution.py:15
  122.0 21.1 %collective-permute-start.3 = (bf16[512,768]{1,0:T(8,128)(2,1)S(1)}, bf16[512,768]{1,0:T(8,128)(2,1)S(1)}, u32[]{:S(2)}, u32[]{:S(2)}) collective-permute-start(bf16[512,768]{1,0:T(8,128)(2,1)S(1)} %collective-permute-done.2), channel_id=1, source_target_pairs={{0,16},{16,32},{32,48},{48,64},{64,80},{80,96},{96,112},{112,0},{1... | collective-permute-start | bytes 2359304 | tf_op jit(solution)/shard_map/ppermute | solution.py:15
  148.3 9.8 %all-to-all-start = ((f32[8,1,512]{2,1,0:T(1,128)}), f32[8,1,512]{2,1,0:T(1,128)S(1)}, u32[]{:S(2)}, u32[]{:S(2)}) async-start(f32[8,1,512]{2,1,0:T(1,128)} %copy.15), calls=%async_computation | async-start | bytes 32768 | tf_op jit(solution)/shard_map/all_to_all | solution.py:66
where the time goes:
time: 162 us; the launch traced here: 159 us
  waiting for transfers between devices  56.6 us (35%)
  matrix products  41.7 us (26%)
  starting transfers between devices  38.8 us (24%)
  other arithmetic  10.7 us (7%)
  between operations  6.13 us (4%)
  local copies, waits for them, and re-layouts  4.88 us (3%)
    ppermute x7, waiting for transfers between devices, shifted(): return lax.ppermute(value, axis, pairs)  50.7 us
    dot_general x8, matrix products, tile_max(): lax.dot_general(rows, index_unit, (((1,), (1,)), ((), ())), preferred_ele...  39.6 us
    ppermute x7, starting transfers between devices, shifted(): return lax.ppermute(value, axis, pairs)  25.5 us
    all_to_all x1, starting transfers between devices, sent_together(): lax.all_to_all(both, axis, split_axis=split_dim, concat_axis=concat_dim,...  9.92 us
    all_to_all x1, waiting for transfers between devices, per_device(): lax.all_to_all(by_anchor, 'blk', split_axis=0, concat_axis=0, tiled=True)  5.9 us
    reduce_sum x2, other arithmetic, unit_rows(): scale = lax.rsqrt(jnp.sum(wide * wide, axis=-1, keepdims=True) + EPS)  5.6 us
    all_to_all x1, starting transfers between devices, per_device(): lax.all_to_all(by_anchor, 'blk', split_axis=0, concat_axis=0, tiled=True)  3.33 us
  transfers between devices with their start and end apart: 9, of which 6 were waited for; matrix products, arithmetic and copies ran while one was open for 30% of the time, Pallas kernels for 0%

commit v1 on v0

--- a/solution.py
+++ b/solution.py
@@ -1,18 +1,19 @@
+import functools
+
 import jax
 import jax.numpy as jnp
 from jax import lax
+from jax.experimental import pallas as pl
+from jax.experimental.pallas import tpu as pltpu
 from jax.sharding import PartitionSpec as P
 
 CL_DEV = 16
-
-
 EPS = 1e-06
-
-
-def shifted(value, axis, steps):
-    count = lax.axis_size(axis)
-    pairs = [(source, (source + steps) % count) for source in range(count)]
-    return lax.ppermute(value, axis, pairs)
+MESH = pl.DeviceIdType.MESH
+ROWS = 512
+CH = 128
+D = 768
+HALF = 2048
 
 
 def sent_together(arrays, axis, split_dim, concat_dim, along):
@@ -34,37 +35,281 @@
     return (wide * scale).astype(jnp.bfloat16)
 
 
+def ring4(v):
+    return lax.rem(v + 4, 4)
+
+
+def quad_at(k):
+    return 2 * ROWS + ROWS * k
+
+
+CROSS_AT = (0, 1, 4, 5)
+XM_AT = (2, 6, 8, 10)
+XP_AT = (3, 7, 9, 11)
+X2_AT = (12, 13, 14, 15)
+
+
+def best_kernel(
+    new_hbm, index_hbm, pattern, out_ref,
+    nr, ir, oi, acc0, acc1, ret_out, ret_in,
+    load_sem, bar_unused,
+    z_s, z_r, z2_s, z2_r, sib_s, sib_r, cr_s, cr_r, x_s, x_r, x2_s, x2_r, ret_s, ret_r,
+):
+    b = lax.axis_index("blk")
+    s = lax.axis_index("slab")
+    z, h = lax.div(b, 2), lax.rem(b, 2)
+    x, l, c = lax.div(s, 4), lax.rem(lax.div(s, 2), 2), lax.rem(s, 2)
+
+    def blk_of(dz, dh=0):
+        return ring4(z + dz) * 2 + (1 - h if dh else h)
+
+    def slab_of(dx=0, dl=0, dc=0):
+        return (ring4(x + dx) * 2 + (1 - l if dl else l)) * 2 + (1 - c if dc else c)
+
+    zp, zm = (blk_of(1), s), (blk_of(-1), s)
+    xp, xm = (b, slab_of(1)), (b, slab_of(-1))
+    sib = (b, slab_of(0, 0, 1))
+    cross = (blk_of(0, 1), slab_of(0, 1, 0))
+    back = [(dz, dc) for dz in (0, 1, 2, 3) for dc in (0, 1) if (dz, dc) != (0, 0)]
+    back_id = [(blk_of(dz), slab_of(0, 0, dc)) for dz, dc in back]
+    partners = [xp, xm, cross] + back_id
+
+    barrier = pltpu.get_barrier_semaphore()
+    for p in partners:
+        pl.semaphore_signal(barrier, inc=1, device_id=p, device_id_type=MESH)
+
+    load_new = pltpu.make_async_copy(new_hbm, nr.at[pl.ds(0, ROWS)], load_sem.at[0])
+    load_new.start()
+    loads = []
+    for j in range(4):
+        u = ring4(x + j)
+        at = pl.multiple_of(u * ROWS, ROWS)
+        cp = pltpu.make_async_copy(
+            index_hbm.at[pl.ds(pl.multiple_of(c * HALF + u * ROWS, ROWS), ROWS)],
+            ir.at[pl.ds(at, ROWS)],
+            load_sem.at[1 + j],
+        )
+        cp.start()
+        loads.append((cp, at))
+
+    def remote(src, dst, ss, rs, dev):
+        return pltpu.make_async_remote_copy(
+            src_ref=src, dst_ref=dst, send_sem=ss, recv_sem=rs, device_id=dev, device_id_type=MESH
+        )
+
+    def rows(ref, at, n=CH):
+        return ref.at[pl.ds(at, n)]
+
+    own_p = [remote(rows(nr, CH * k), rows(nr, quad_at(k)), z_s.at[0, k], z_r.at[0, k], zp) for k in range(4)]
+    own_m = [
+        remote(rows(nr, CH * ((k + 2) % 4)), rows(nr, quad_at(k) + CH), z_s.at[1, k], z_r.at[1, k], zm)
+        for k in range(4)
+    ]
+    fwd_p = [remote(rows(nr, quad_at(k)), rows(nr, quad_at(4 + k)), z2_s.at[0, k], z2_r.at[0, k], zp) for k in range(2)]
+    fwd_m = [
+        remote(rows(nr, quad_at(k) + CH), rows(nr, quad_at(4 + k) + CH), z2_s.at[1, k], z2_r.at[1, k], zm)
+        for k in range(2)
+    ]
+    to_sib = [remote(rows(nr, 0, ROWS), rows(nr, ROWS, ROWS), sib_s.at[6], sib_r.at[6], sib)]
+    pair_sib = [
+        remote(rows(nr, quad_at(k), 2 * CH), rows(nr, quad_at(k) + 2 * CH, 2 * CH), sib_s.at[k], sib_r.at[k], sib)
+        for k in range(6)
+    ]
+    cr = [
+        remote(
+            ir.at[pl.ds(pl.multiple_of(x * ROWS + CH * k, CH), CH)],
+            rows(oi, CH * CROSS_AT[k]), cr_s.at[k], cr_r.at[k], cross,
+        )
+        for k in range(4)
+    ]
+    x_p = [remote(rows(oi, CH * CROSS_AT[k]), rows(oi, CH * XM_AT[k]), x_s.at[0, k], x_r.at[0, k], xp) for k in range(4)]
+    x_m = [remote(rows(oi, CH * CROSS_AT[k]), rows(oi, CH * XP_AT[k]), x_s.at[1, k], x_r.at[1, k], xm) for k in range(4)]
+    x_f = [
+        remote(rows(oi, CH * XM_AT[k]), rows(oi, CH * X2_AT[k]), x2_s.at[k], x2_r.at[k], xp)
+        if k % 2 == 0
+        else remote(rows(oi, CH * XP_AT[k]), rows(oi, CH * X2_AT[k]), x2_s.at[k], x2_r.at[k], xm)
+        for k in range(4)
+    ]
+
+    acc0[...] = jnp.full(acc0.shape, -3.0, jnp.float32)
+    acc1[...] = jnp.full(acc1.shape, -3.0, jnp.float32)
+
+    def normalize(ref, at, n=CH):
+        ref[pl.ds(at, n), :] = unit_rows(ref[pl.ds(at, n), :])
+
+    load_new.wait()
+    normalize(nr, 0)
+    normalize(nr, 2 * CH)
+    pl.semaphore_wait(barrier, len(partners))
+    own_p[0].start()
+    own_m[0].start()
+    normalize(nr, CH)
+    normalize(nr, 3 * CH)
+    for k in range(1, 4):
+        own_p[k].start()
+        own_m[k].start()
+    to_sib[0].start()
+
+    loads[0][0].wait()
+    for k in range(4):
+        normalize(ir, pl.multiple_of(x * ROWS + CH * k, CH))
+        cr[k].start()
+    for cp, at in loads[1:]:
+        cp.wait()
+        for k in range(4):
+            normalize(ir, pl.multiple_of(at + CH * k, CH))
+
+    def scores(acc, idx, i_at, i_n, n_at, n_n):
+        prod = lax.dot_general(
+            idx[pl.ds(i_at, i_n), :], nr[pl.ds(n_at, n_n), :],
+            (((1,), (1,)), ((), ())), preferred_element_type=jnp.float32,
+        )
+        top = jnp.max(prod.reshape(i_n // 8, 8, n_n), axis=0)
+        acc[:, pl.ds(n_at, n_n)] = jnp.maximum(acc[:, pl.ds(n_at, n_n)], top)
+
+    def own_range(n_at):
+        scores(acc0, ir, 0, HALF, n_at, ROWS)
+
+    def other_range(g, half):
+        scores(acc1, oi, ROWS * g, ROWS, HALF * half, HALF)
+
+    own_range(0)
+    to_sib[0].wait_recv()
+    own_range(ROWS)
+
+    def z_in(k):
+        if k < 4:
+            own_p[k].wait_recv()
+            if k < 2:
+                fwd_p[k].start()
+            own_m[k].wait_recv()
+            if k < 2:
+                fwd_m[k].start()
+        else:
+            fwd_p[k - 4].wait_recv()
+            fwd_m[k - 4].wait_recv()
+        pair_sib[k].start()
+
+    def cross_in(k):
+        cr[k].wait_recv()
+        x_p[k].start()
+        x_m[k].start()
+
+    def x_in(k):
+        x_p[k].wait_recv()
+        if k % 2 == 0:
+            x_f[k].start()
+        x_m[k].wait_recv()
+        if k % 2 == 1:
+            x_f[k].start()
+
+    def quad(k):
+        pair_sib[k].wait_recv()
+        own_range(quad_at(k))
+
+    z_in(0)
+    cross_in(0)
+    quad(0)
+    z_in(1)
+    cross_in(1)
+    x_in(0)
+    quad(1)
+    z_in(2)
+    cross_in(2)
+    x_in(1)
+    quad(2)
+    other_range(0, 0)
+    z_in(3)
+    cross_in(3)
+    quad(3)
+    x_in(2)
+    other_range(1, 0)
+    z_in(4)
+    x_in(3)
+    quad(4)
+    other_range(2, 0)
+    z_in(5)
+    quad(5)
+    other_range(0, 1)
+    other_range(1, 1)
+    other_range(2, 1)
+    for k in range(4):
+        x_f[k].wait_recv()
+    other_range(3, 0)
+    other_range(3, 1)
+
+    def block_best(dz, dc):
+        side = 2 * CH * dc
+        if dz == 0:
+            where = [ROWS * dc + CH * q for q in range(4)]
+        elif dz == 3:
+            where = [quad_at(q) + side for q in range(4)]
+        elif dz == 1:
+            where = [quad_at((q + 2) % 4) + side + CH for q in range(4)]
+        else:
+            where = [quad_at(4 + q % 2) + side + CH * (q // 2) for q in range(4)]
+        row = blk_of(dz) * 16 + slab_of(0, 0, dc)
+        live0 = jnp.full((1, ROWS), pattern[row, b], jnp.int32) > 0
+        live1 = jnp.full((1, ROWS), pattern[row, blk_of(0, 1)], jnp.int32) > 0
+
+        def top(acc):
+            parts = [jnp.max(acc[:, pl.ds(w, CH)], axis=0, keepdims=True) for w in where]
+            return jnp.concatenate(parts, axis=1)
+
+        return jnp.maximum(jnp.where(live0, top(acc0), -2.0), jnp.where(live1, top(acc1), -2.0))
+
+    rets = []
+    for i, (dz, dc) in enumerate(back):
+        ret_out[i] = block_best(dz, dc)
+        cp = remote(ret_out.at[i], ret_in.at[i], ret_s.at[i], ret_r.at[i], back_id[i])
+        cp.start()
+        rets.append(cp)
+    best = block_best(0, 0)
+    for cp in rets:
+        cp.wait_recv()
+    for i in range(len(back)):
+        best = jnp.maximum(best, ret_in[i])
+    out_ref[...] = best
+    for cp in own_p + own_m + fwd_p + fwd_m + to_sib + pair_sib + cr + x_p + x_m + x_f + rets:
+        cp.wait_send()
+
+
+def best_of(new_rows, index_rows, pattern):
+    dma = pltpu.SemaphoreType.DMA
+    return pl.pallas_call(
+        best_kernel,
+        out_shape=jax.ShapeDtypeStruct((1, ROWS), jnp.float32),
+        in_specs=[
+            pl.BlockSpec(memory_space=pl.ANY),
+            pl.BlockSpec(memory_space=pl.ANY),
+            pl.BlockSpec(memory_space=pltpu.SMEM),
+        ],
+        out_specs=pl.BlockSpec(memory_space=pltpu.VMEM),
+        scratch_shapes=[
+            pltpu.VMEM((8 * ROWS, D), jnp.bfloat16),
+            pltpu.VMEM((HALF, D), jnp.bfloat16),
+            pltpu.VMEM((HALF, D), jnp.bfloat16),
+            pltpu.VMEM((8, 8 * ROWS), jnp.float32),
+            pltpu.VMEM((8, 8 * ROWS), jnp.float32),
+            pltpu.VMEM((7, 1, ROWS), jnp.float32),
+            pltpu.VMEM((7, 1, ROWS), jnp.float32),
+            dma((5,)),
+            dma((1,)),
+            dma((2, 4)), dma((2, 4)), dma((2, 2)), dma((2, 2)), dma((7,)), dma((7,)),
+            dma((4,)), dma((4,)), dma((2, 4)), dma((2, 4)), dma((4,)), dma((4,)), dma((7,)), dma((7,)),
+        ],
+        compiler_params=pltpu.CompilerParams(
+            collective_id=0, has_side_effects=True, vmem_limit_bytes=56 << 20
+        ),
+        cost_estimate=pl.CostEstimate(flops=2 * 8 * 512 * 4096 * 768, bytes_accessed=10 << 20, transcendentals=0),
+    )(new_rows, index_rows, pattern).reshape(ROWS)
+
+
 def per_device(new_rows, index_rows, pattern, kept_row, kept_owner, kept_local):
     cycle = lax.axis_size("blk")
     lanes = lax.axis_size("slab")
-    here = lax.axis_index("blk")
-    lane = lax.axis_index("slab")
+    best = best_of(new_rows, index_rows, pattern)
     new_unit = unit_rows(new_rows)
-    index_unit = unit_rows(index_rows)
-
-    def tile_max(rows, offset):
-        anchor = (here - offset) % cycle
-        active = pattern[anchor * lanes + lane, here] > 0
-        scores = lax.dot_general(
-            rows, index_unit, (((1,), (1,)), ((), ())), preferred_element_type=jnp.float32
-        )
-        return jnp.where(active, jnp.max(scores, axis=1), jnp.float32(-2.0))
-
-    slots = {0: tile_max(new_unit, 0)}
-    ahead_steps = cycle // 2
-    moving = new_unit
-    for step in range(1, ahead_steps + 1):
-        moving = shifted(moving, "blk", 1)
-        slots[step] = tile_max(moving, step)
-    behind = new_unit
-    for step in range(1, cycle - ahead_steps):
-        behind = shifted(behind, "blk", -1)
-        slots[cycle - step] = tile_max(behind, cycle - step)
-    stacked = jnp.stack([slots[offset] for offset in range(cycle)], axis=0)
-    order = (here - jnp.arange(cycle, dtype=jnp.int32)) % cycle
-    by_anchor = jnp.take(stacked, order, axis=0)
-    returned = lax.all_to_all(by_anchor, "blk", split_axis=0, concat_axis=0, tiled=True)
-    best = jnp.max(returned, axis=0)
     picked = new_unit[kept_row]
     owner = kept_owner[:, 0]
     devices = cycle * lanes

time: 162 us -> 86.8 us (0.54); the launches traced: 159 us -> 86.4 us
  Pallas kernels: 0 us -> 63.2 us
  waiting for transfers between devices: 56.6 us -> 0.01 us
  matrix products: 41.7 us -> 1.49 us
  starting transfers between devices: 38.8 us -> 11.7 us
  other arithmetic: 10.7 us -> 4.99 us
  between operations: 6.13 us -> 0.77 us
    pallas_call x0 -> x1, Pallas kernels: none -> 63.2 us  [best_of(): pl.pallas_call(best_kernel, out_shape=jax.ShapeDtypeStruct((1, ROWS), jnp...]
    ppermute x7 -> x0, waiting for transfers between devices: 50.7 us -> none  [shifted(): return lax.ppermute(value, axis, pairs)]
    dot_general x8 -> x0, matrix products: 39.6 us -> none  [tile_max(): lax.dot_general(rows, index_unit, (((1,), (1,)), ((), ())), preferred_ele...]
    ppermute x7 -> x0, starting transfers between devices: 25.5 us -> none  [shifted(): return lax.ppermute(value, axis, pairs)]
    all_to_all x1 -> x0, waiting for transfers between devices: 5.9 us -> none  [per_device(): lax.all_to_all(by_anchor, 'blk', split_axis=0, concat_axis=0, tiled=True)]
    reduce_sum x2 -> x1, other arithmetic: 5.6 us -> 1.36 us  [unit_rows(): scale = lax.rsqrt(jnp.sum(wide * wide, axis=-1, keepdims=True) + EPS)]
    all_to_all x1 -> x0, starting transfers between devices: 3.33 us -> none  [per_device(): lax.all_to_all(by_anchor, 'blk', split_axis=0, concat_axis=0, tiled=True)]
    all_to_all x1, starting transfers between devices: 9.92 us -> 11.7 us  [sent_together(): lax.all_to_all(both, axis, split_axis=split_dim, concat_axis=concat_dim,...]
  transfers between devices with their start and end apart: 9 -> 1, of which waited for: 6 -> 0; matrix products, arithmetic and copies ran while one was open for 30% -> 1% of each run, Pallas kernels for 0% -> 73%
where the time goes in v1:
time: 86.8 us; the launch traced here: 86.4 us
  Pallas kernels  63.2 us (73%)
  starting transfers between devices  11.7 us (13%)
  other arithmetic  4.99 us (6%)
  local copies, waits for them, and re-layouts  4.25 us (5%)
  matrix products  1.49 us (2%)
    pallas_call x1, Pallas kernels, best_of(): pl.pallas_call(best_kernel, out_shape=jax.ShapeDtypeStruct((1, ROWS), jnp...  63.2 us
    all_to_all x1, starting transfers between devices, sent_together(): lax.all_to_all(both, axis, split_axis=split_dim, concat_axis=concat_dim,...  11.7 us
  transfers between devices with their start and end apart: 1, of which 0 were waited for; matrix products, arithmetic and copies ran while one was open for 1% of the time, Pallas kernels for 73%

profile of v1, /device:TPU:1, one launch (start us, length us, event | category | flops | bytes accessed | tf_op | source)
XLA Modules:
  0.0 86.4 jit_solution(10193707154410908452)
XLA Ops:
  0.6 0.0 copy-start.2
  0.6 0.9 %convert_reduce_fusion.1 = s32[256]{0:T(256)S(1)} fusion(s32[256]{0:T(256)} %bitcast.3), kind=kLoop, calls=%fused_computation.14 | loop fusion | flops 327424 | bytes 2048 | tf_op jit(solution)/shard_map/reduce_sum | solution.py:324
  1.6 0.7 multiply_add_fusion
  2.3 1.4 %fusion = f32[512]{0:T(512)S(1)} fusion(bf16[512,768]{1,0:T(8,128)(2,1)} %new_hbm.1), kind=kLoop, calls=%fused_computation.3 | loop fusion | flops 1179136 | bytes 788480 | tf_op jit(solution)/shard_map/reduce_sum | solution.py:34
  3.6 1.3 %fusion.1 = bf16[512,768]{1,0:T(8,128)(2,1)S(1)} fusion(bf16[512,768]{1,0:T(8,128)(2,1)} %new_hbm.1, f32[512]{0:T(512)S(1)} %add_rsqrt_fusion), kind=kLoop, calls=%fused_computation.4 | loop fusion | flops 1179648 | bytes 1574912 | tf_op jit(solution)/shard_map/convert_element_type | solution.py:35
  5.0 0.0 copy-done.2
  5.0 0.0 copy-start.3
  5.0 1.2 %gather_fusion = bf16[256,768]{1,0:T(8,128)(2,1)S(1)} fusion(bf16[512,768]{1,0:T(8,128)(2,1)S(1)} %fusion.1, s32[1024]{0:T(1024)S(1)} %pad_clamp_fusion), kind=kCustom, calls=%fused_computation | custom fusion | bytes 787456 | tf_op jit(solution)/shard_map/gather | solution.py:313
  6.2 0.4 convolution_convert_fusion
  6.6 0.0 copy-done.3
  6.6 0.3 convolution_convert_fusion.1
  6.9 0.1 copy.16
  7.0 0.1 pad_maximum_fusion
  7.1 0.0 copy-start
  7.1 1.2 %all_to_all.8 = bf16[128,4,784]{2,1,0:T(4,128)(2,1)} reshape(bf16[512,784]{1,0:T(8,128)(2,1)S(1)} %pad_maximum_fusion) | data formatting | bytes 1605632 | tf_op jit(solution)/shard_map/all_to_all | solution.py:22
  8.2 11.7 %all-to-all-start = ((bf16[128,4,784]{2,1,0:T(4,128)(2,1)}), bf16[128,4,784]{2,1,0:T(4,128)(2,1)S(1)}, u32[]{:S(2)}, u32[]{:S(2)}) async-start(bf16[128,4,784]{2,1,0:T(4,128)(2,1)} %all_to_all.8), calls=%async_computation | async-start | bytes 1835008 | tf_op jit(solution)/shard_map/all_to_all | solution.py:22
  19.9 0.0 copy-done
  19.9 0.7 copy.15.pattern
  20.6 63.2 %shard_map.85 = f32[1,512]{1,0:T(1,128)} custom-call(bf16[512,768]{1,0:T(8,128)(2,1)} %new_hbm.1, bf16[4096,768]{1,0:T(8,128)(2,1)} %index_hbm.1, s32[128,8]{1,0:T(8,128)} %copy.15.pattern), custom_call_target="tpu_custom_call" | custom-call | flops 25769803776 | bytes 10485760 | tf_op jit(solution)/shard_map/pallas_call | solution.py:279
  83.9 0.0 copy-start.1
  83.9 0.0 all-to-all-done
  83.9 0.5 all_to_all.10
  84.4 0.9 fusion.2
  85.2 0.6 convert_reduce_fusion
  85.8 0.0 copy-done.1
  85.8 0.6 copy.18
  (3 shorter events, 0.0 us)
Async XLA Ops:
  0.6 4.3 %copy-start.2 = (s32[256]{0:T(256)S(1)}, s32[256]{0:T(256)}, u32[]{:S(2)}) copy-start(s32[256]{0:T(256)} %param.9) | copy-start | bytes 3076
  5.0 1.6 %copy-start.3 = (s32[256]{0:T(256)S(1)}, s32[256]{0:T(256)}, u32[]{:S(2)}) copy-start(s32[256]{0:T(256)} %param.11) | copy-start | bytes 3076
  7.1 12.9 %copy-start = (s32[128,8]{0,1:T(8,128)S(1)}, s32[128,8]{0,1:T(8,128)}, u32[]{:S(2)}) copy-start(s32[128,8]{0,1:T(8,128)} %param.8) | copy-start | bytes 12292
  8.2 75.7 %all-to-all-start = ((bf16[128,4,784]{2,1,0:T(4,128)(2,1)}), bf16[128,4,784]{2,1,0:T(4,128)(2,1)S(1)}, u32[]{:S(2)}, u32[]{:S(2)}) async-start(bf16[128,4,784]{2,1,0:T(4,128)(2,1)} %all_to_all.8), calls=%async_computation | async-start | bytes 1835008 | tf_op jit(solution)/shard_map/all_to_all | solution.py:22
  83.9 1.9 %copy-start.1 = (f32[1,512]{1,0:T(1,128)S(1)}, f32[1,512]{1,0:T(1,128)}, u32[]{:S(2)}) copy-start(f32[1,512]{1,0:T(1,128)} %shard_map.85) | copy-start | bytes 6148

commit v2 on v1

v2 whole, which is shorter than its diff:
```python
import jax
import jax.numpy as jnp
from jax import lax
from jax.experimental import pallas as pl
from jax.experimental.pallas import tpu as pltpu
from jax.sharding import PartitionSpec as P

CL_DEV = 16
EPS = 1e-06
MESH = pl.DeviceIdType.MESH
ROWS = 512
KEEP = 256
CH = 128
D = 768
HALF = 2048
UC = 96
UNIT = 4 * UC
COMMON = 512
WIDE = D + 128
PLANE = 256


def unit_rows(values):
    wide = values.astype(jnp.float32)
    scale = lax.rsqrt(jnp.sum(wide * wide, axis=-1, keepdims=True) + EPS)
    return (wide * scale).astype(jnp.bfloat16)


def ring4(v):
    return lax.rem(v + 4, 4)


def quad_at(k):
    return 2 * ROWS + ROWS * k


def places(dz, dc):
    side = 2 * CH * dc
    if dz == 0:
        return [ROWS * dc + CH * q for q in range(4)]
    if dz == 3:
        return [quad_at(q) + side for q in range(4)]
    if dz == 1:
        return [quad_at((q + 2) % 4) + side + CH for q in range(4)]
    return [quad_at(4 + q % 2) + side + CH * (q // 2) for q in range(4)]


CR_AT = (0, UC, 4 * UC, 5 * UC)
XM_AT = (2 * UC, 6 * UC, 8 * UC, 10 * UC)
XP_AT = (3 * UC, 7 * UC, 9 * UC, 11 * UC)
X2_AT = (12 * UC, 13 * UC, 14 * UC, 15 * UC)
AC_AT = (16 * UC, 16 * UC + CH)
AY_AT = (16 * UC + 2 * CH, 16 * UC + 3 * CH)


def window_kernel(
    new_hbm, index_hbm, pattern_hbm, row_hbm, owner_hbm, local_hbm, best_ref, sums_ref, counts_ref,
    nr, ir, oi, acc0, acc1, ret_out, ret_in, pattern, kept, codes, weights, partial, got,
    load_sem, z_s, z_r, z2_s, z2_r, sib_s, sib_r, cr_s, cr_r, ac_s, ac_r, ay_s, ay_r,
    x_s, x_r, x2_s, x2_r, ret_s, ret_r, code_s, code_r, sum_s, sum_r,
):
    b = lax.axis_index("blk")
    s = lax.axis_index("slab")
    z, h = lax.div(b, 2), lax.rem(b, 2)
    x, l, c = lax.div(s, 4), lax.rem(lax.div(s, 2), 2), lax.rem(s, 2)

    def blk_of(dz, dh=0):
        return ring4(z + dz) * 2 + (1 - h if dh else h)

    def slab_of(dx=0, dl=0, dc=0):
        return (ring4(x + dx) * 2 + (1 - l if dl else l)) * 2 + (1 - c if dc else c)

    zp, zm = (blk_of(1), s), (blk_of(-1), s)
    xp, xm = (b, slab_of(1)), (b, slab_of(-1))
    sib = (b, slab_of(0, 0, 1))
    cross = (blk_of(0, 1), slab_of(0, 1, 0))
    ylo = (b, slab_of(0, 1, 0))
    back = [(dz, dc) for dz in (0, 1, 2, 3) for dc in (0, 1) if (dz, dc) != (0, 0)]
    back_id = [(blk_of(dz), slab_of(0, 0, dc)) for dz, dc in back]
    plane = [(dh, dx, dl) for dx in (0, 1, 3, 2) for dh in (0, 1) for dl in (0, 1) if (dh, dx, dl) != (0, 0, 0)]
    plane_id = [(blk_of(0, dh), slab_of(dx, dl)) for dh, dx, dl in plane]
    partners = back_id + plane_id

    barrier = pltpu.get_barrier_semaphore()
    for p in partners:
        pl.semaphore_signal(barrier, inc=1, device_id=p, device_id_type=MESH)

    def rows(ref, at, n=CH):
        return ref.at[pl.ds(at, n)]

    loads = [pltpu.make_async_copy(new_hbm, rows(nr, 0, ROWS), load_sem.at[0])]
    half_to = pl.multiple_of((1 - l) * (COMMON // 2), 128)
    half_here = pl.multiple_of(l * (COMMON // 2), 128)
    index_parts = [(pl.multiple_of(COMMON + x * UNIT, 128), UNIT), (half_to, COMMON // 2), (half_here, COMMON // 2)]
    index_parts += [(pl.multiple_of(COMMON + ring4(x + j) * UNIT, 128), UNIT) for j in (1, 2, 3)]
    for j, (at, n) in enumerate(index_parts):
        loads.append(
            pltpu.make_async_copy(
                index_hbm.at[pl.ds(pl.multiple_of(c * HALF + at, 128), n)], rows(ir, at, n), load_sem.at[1 + j]
            )
        )
    small = [
        pltpu.make_async_copy(ref, kept.at[j], load_sem.at[7 + j])
        for j, ref in enumerate((row_hbm, owner_hbm, local_hbm))
    ]
    small.append(pltpu.make_async_copy(pattern_hbm, pattern, load_sem.at[10]))
    for cp in loads + small:
        cp.start()

    def remote(src, dst, ss, rs, dev):
        return pltpu.make_async_remote_copy(
            src_ref=src, dst_ref=dst, send_sem=ss, recv_sem=rs, device_id=dev, device_id_type=MESH
        )

    own_p = [remote(rows(nr, CH * k), rows(nr, quad_at(k)), z_s.at[0, k], z_r.at[0, k], zp) for k in range(4)]
    own_m = [
        remote(rows(nr, CH * ((k + 2) % 4)), rows(nr, quad_at(k) + CH), z_s.at[1, k], z_r.at[1, k], zm)
        for k in range(4)
    ]
    fwd_p = [remote(rows(nr, quad_at(k)), rows(nr, quad_at(4 + k)), z2_s.at[0, k], z2_r.at[0, k], zp) for k in range(2)]
    fwd_m = [
        remote(rows(nr, quad_at(k) + CH), rows(nr, quad_at(4 + k) + CH), z2_s.at[1, k], z2_r.at[1, k], zm)
        for k in range(2)
    ]
    to_sib = [remote(rows(nr, 0, ROWS), rows(nr, ROWS, ROWS), sib_s.at[6], sib_r.at[6], sib)]
    pair_sib = [
        remote(rows(nr, quad_at(k), 2 * CH), rows(nr, quad_at(k) + 2 * CH, 2 * CH), sib_s.at[k], sib_r.at[k], sib)
        for k in range(6)
    ]
    unit_at = [pl.multiple_of(COMMON + x * UNIT + UC * k, 32) for k in range(4)]
    cr = [remote(rows(ir, unit_at[k], UC), rows(oi, CR_AT[k], UC), cr_s.at[k], cr_r.at[k], cross) for k in range(4)]
    common_at = [pl.multiple_of(half_to + CH * k, CH) for k in range(2)]
    ac = [remote(rows(ir, common_at[k]), rows(oi, AC_AT[k]), ac_s.at[k], ac_r.at[k], cross) for k in range(2)]
    ay = [remote(rows(oi, AC_AT[k]), rows(oi, AY_AT[k]), ay_s.at[k], ay_r.at[k], ylo) for k in range(2)]
    x_p = [remote(rows(oi, CR_AT[k], UC), rows(oi, XM_AT[k], UC), x_s.at[0, k], x_r.at[0, k], xp) for k in range(4)]
    x_m = [remote(rows(oi, CR_AT[k], UC), rows(oi, XP_AT[k], UC), x_s.at[1, k], x_r.at[1, k], xm) for k in range(4)]
    x_f = [
        remote(rows(oi, (XP_AT if k % 2 else XM_AT)[k], UC), rows(oi, X2_AT[k], UC), x2_s.at[k], x2_r.at[k], xm if k % 2 else xp)
        for k in range(4)
    ]
    code = [remote(codes.at[0], codes.at[1 + i], code_s.at[i], code_r.at[i], dev) for i, dev in enumerate(back_id)]

    def place_of(dh, dx, dl):
        return (1 - h if dh else h) * 8 + ring4(x + dx) * 2 + (1 - l if dl else l)

    def cluster_rows(dh, dx, dl):
        return pl.ds(pl.multiple_of(place_of(dh, dx, dl) * CL_DEV, CL_DEV), CL_DEV)

    sums = [
        remote(partial.at[cluster_rows(*plane[j])], got.at[j], sum_s.at[j], sum_r.at[j], plane_id[j])
        for j in range(len(plane))
    ]

    acc0[...] = jnp.full(acc0.shape, -3.0, jnp.float32)
    acc1[...] = jnp.full(acc1.shape, -3.0, jnp.float32)

    def normalize(ref, at, n=CH):
        ref[pl.ds(at, n), :] = unit_rows(ref[pl.ds(at, n), :])

    loads[0].wait()
    normalize(nr, 0)
    normalize(nr, 2 * CH)
    normalize(nr, CH)
    normalize(nr, 3 * CH)
    loads[1].wait()
    for k in range(4):
        normalize(ir, unit_at[k], UC)
    for cp in small:
        cp.wait()
    codes[0] = (kept[1] * CL_DEV + kept[2]) * ROWS + kept[0]
    pl.semaphore_wait(barrier, len(partners))
    for k in range(4):
        own_p[k].start()
        own_m[k].start()
        cr[k].start()
    to_sib[0].start()
    for cp in code:
        cp.start()
    loads[2].wait()
    for k in range(2):
        normalize(ir, common_at[k])
        ac[k].start()
    for j in range(2, 6):
        loads[1 + j].wait()
        at, n = index_parts[j]
        for k in range(n // CH):
            normalize(ir, pl.multiple_of(at + CH * k, CH))

    def scores(acc, idx, i_at, i_n, n_at, n_n):
        prod = lax.dot_general(
            idx[pl.ds(i_at, i_n), :], nr[pl.ds(n_at, n_n), :],
            (((1,), (1,)), ((), ())), preferred_element_type=jnp.float32,
        )
        top = jnp.max(prod.reshape(i_n // 8, 8, n_n), axis=0)
        acc[:, pl.ds(n_at, n_n)] = jnp.maximum(acc[:, pl.ds(n_at, n_n)], top)

    def own_range(n_at):
        scores(acc0, ir, 0, HALF, n_at, ROWS)

    def other_range(i_at, i_end, n_at, n_end):
        scores(acc1, oi, i_at, i_end - i_at, n_at, n_end - n_at)

    def z_in(k):
        if k < 4:
            own_p[k].wait_recv()
            if k < 2:
                fwd_p[k].start()
            own_m[k].wait_recv()
            if k < 2:
                fwd_m[k].start()
        else:
            fwd_p[k - 4].wait_recv()
            fwd_m[k - 4].wait_recv()
        pair_sib[k].start()

    def cross_in(k):
        cr[k].wait_recv()
        x_p[k].start()
        x_m[k].start()

    def common_in(k):
        ac[k].wait_recv()
        ay[k].start()

    def x_in(k):
        x_p[k].wait_recv()
        if k % 2 == 0:
            x_f[k].start()
        x_m[k].wait_recv()
        if k % 2 == 1:
            x_f[k].start()

    def quad(k):
        pair_sib[k].wait_recv()
        own_range(quad_at(k))

    def weigh(slot, dz, dc):
        both = codes[slot]
        row = lax.rem(both, ROWS)
        local = lax.rem(lax.div(both, ROWS), CL_DEV)
        owner = lax.div(both, ROWS * CL_DEV)
        o_blk, o_slab = lax.div(owner, 16), lax.rem(owner, 16)
        mine = (lax.div(o_blk, 2) == z) & (lax.rem(o_slab, 2) == c)
        cluster = (lax.rem(o_blk, 2) * 8 + lax.div(o_slab, 2)) * CL_DEV + local
        cluster = jnp.where(mine, cluster, -1)

        def hot(count, which):
            at = lax.broadcasted_iota(jnp.int32, (count, KEEP), 0)
            return jnp.where(at == which, 1.0, 0.0).astype(jnp.bfloat16)

        named = lax.dot_general(
            hot(PLANE, cluster), hot(ROWS, row), (((1,), (1,)), ((), ())), preferred_element_type=jnp.float32
        )
        for q, at in enumerate(places(dz, dc)):
            weights[:, pl.ds(at, CH)] = named[:, CH * q : CH * (q + 1)].astype(jnp.bfloat16)
        return jnp.sum(named, axis=1, keepdims=True)

    def add_rows(n_at, n_end, first):
        part = jnp.dot(
            weights[:, pl.ds(n_at, n_end - n_at)], nr[pl.ds(n_at, n_end - n_at), :], preferred_element_type=jnp.float32
        )
        partial[:, pl.ds(0, D)] = part if first else partial[:, pl.ds(0, D)] + part

    own_range(0)
    to_sib[0].wait_recv()
    own_range(ROWS)
    cross_in(0)
    z_in(0)
    count = weigh(0, 0, 0)
    for i, (dz, dc) in enumerate(back):
        code[i].wait_recv()
        count = count + weigh(1 + i, (4 - dz) % 4, dc)
        if i == 3:
            cross_in(1)
    partial[:, pl.ds(D, 128)] = jnp.broadcast_to(count, (PLANE, 128))
    quad(0)
    x_in(0)
    z_in(1)
    cross_in(2)
    quad(1)
    x_in(1)
    cross_in(3)
    other_range(0, 4 * UC, 0, 2048)
    z_in(2)
    quad(2)
    x_in(2)
    other_range(4 * UC, 8 * UC, 0, 2048)
    z_in(3)
    common_in(0)
    quad(3)
    x_in(3)
    other_range(0, 8 * UC, 2048, 3072)
    common_in(1)
    other_range(8 * UC, 12 * UC, 0, 3072)
    add_rows(0, 3072, True)
    z_in(4)
    quad(4)
    for k in range(4):
        x_f[k].wait_recv()
    other_range(12 * UC, 16 * UC + 2 * CH, 0, 3072)
    z_in(5)
    pair_sib[5].wait_recv()
    add_rows(3072, 4096, False)
    for cp in sums:
        cp.start()
    own_range(quad_at(5))
    other_range(0, 16 * UC + 2 * CH, 3072, 4096)
    for cp in ay:
        cp.wait_recv()
    other_range(16 * UC + 2 * CH, HALF, 0, 4096)

    def block_best(dz, dc):
        row = blk_of(dz) * 16 + slab_of(0, 0, dc)
        live0 = jnp.full((1, ROWS), pattern[b, row], jnp.int32) > 0
        live1 = jnp.full((1, ROWS), pattern[blk_of(0, 1), row], jnp.int32) > 0

        def top(acc):
            parts = [jnp.max(acc[:, pl.ds(w, CH)], axis=0, keepdims=True) for w in places(dz, dc)]
            return jnp.concatenate(parts, axis=1)

        return jnp.maximum(jnp.where(live0, top(acc0), -2.0), jnp.where(live1, top(acc1), -2.0))

    rets = []
    for i, (dz, dc) in enumerate(back):
        ret_out[i] = block_best(dz, dc)
        cp = remote(ret_out.at[i], ret_in.at[i], ret_s.at[i], ret_r.at[i], back_id[i])
        cp.start()
        rets.append(cp)
    best = block_best(0, 0)
    total = partial[cluster_rows(0, 0, 0), :]
    for j, cp in enumerate(sums):
        cp.wait_recv()
        total = total + got[j]
    sums_ref[...] = total[:, :D]
    counts_ref[...] = total[:, D:]
    for i, cp in enumerate(rets):
        cp.wait_recv()
        best = jnp.maximum(best, ret_in[i])
    best_ref[...] = best
    for cp in own_p + own_m + fwd_p + fwd_m + to_sib + pair_sib + cr + ac + ay + x_p + x_m + x_f + code + sums + rets:
        cp.wait_send()


def per_device(new_rows, index_rows, pattern, kept_row, kept_owner, kept_local):
    dma = pltpu.SemaphoreType.DMA
    f32, bf16, i32 = jnp.float32, jnp.bfloat16, jnp.int32
    best, sums, counts = pl.pallas_call(
        window_kernel,
        out_shape=(
            jax.ShapeDtypeStruct((1, ROWS), f32),
            jax.ShapeDtypeStruct((CL_DEV, D), f32),
            jax.ShapeDtypeStruct((CL_DEV, 128), f32),
        ),
        in_specs=[pl.BlockSpec(memory_space=pl.ANY)] * 6,
        out_specs=[pl.BlockSpec(memory_space=pltpu.VMEM)] * 3,
        scratch_shapes=[
            pltpu.VMEM((8 * ROWS, D), bf16),
            pltpu.VMEM((HALF, D), bf16),
            pltpu.VMEM((HALF, D), bf16),
            pltpu.VMEM((8, 8 * ROWS), f32),
            pltpu.VMEM((8, 8 * ROWS), f32),
            pltpu.VMEM((7, 1, ROWS), f32),
            pltpu.VMEM((7, 1, ROWS), f32),
            pltpu.SMEM((8, 128), i32),
            pltpu.VMEM((3, 1, KEEP), i32),
            pltpu.VMEM((8, 1, KEEP), i32),
            pltpu.VMEM((PLANE, 8 * ROWS), bf16),
            pltpu.VMEM((PLANE, WIDE), f32),
            pltpu.VMEM((15, CL_DEV, WIDE), f32),
            dma((11,)),
            dma((2, 4)), dma((2, 4)), dma((2, 2)), dma((2, 2)), dma((7,)), dma((7,)), dma((4,)), dma((4,)),
            dma((2,)), dma((2,)), dma((2,)), dma((2,)),
            dma((2, 4)), dma((2, 4)), dma((4,)), dma((4,)), dma((7,)), dma((7,)), dma((7,)), dma((7,)),
            dma((15,)), dma((15,)),
        ],
        compiler_params=pltpu.CompilerParams(
            collective_id=0, has_side_effects=True, vmem_limit_bytes=56 << 20
        ),
        cost_estimate=pl.CostEstimate(flops=2 * 8 * 512 * 4096 * 768, bytes_accessed=10 << 20, transcendentals=0),
    )(
        new_rows,
        index_rows,
        pattern.T,
        kept_row.reshape(1, KEEP),
        kept_owner.reshape(1, KEEP),
        kept_local.reshape(1, KEEP),
    )
    return (best.reshape(ROWS), sums, counts[:, 0])


def solution(mesh):
    placed = (
        P(("blk", "slab"), None),
        P("blk", None),
        P(),
        P(("blk", "slab")),
        P(("blk", "slab"), None),
        P(("blk", "slab")),
    )
    return jax.shard_map(
        per_device,
        mesh=mesh,
        in_specs=placed,
        out_specs=(P(("blk", "slab")), P(("blk", "slab"), None), P(("blk", "slab"))),
        check_vma=False,
    )
```

time: 86.8 us -> 80.6 us (0.929)
  Pallas kernels: 63.2 us -> 75.8 us
  starting transfers between devices: 11.7 us -> 0 us
  other arithmetic: 4.99 us -> 0 us
  matrix products: 1.49 us -> 0 us
    pallas_call x1, Pallas kernels: 63.2 us -> 75.8 us  [per_device(): pl.pallas_call(window_kernel, out_shape=(jax.ShapeDtypeStruct((1, ROWS),...]
    all_to_all x1 -> x0, starting transfers between devices: 11.7 us -> none  [sent_together(): lax.all_to_all(both, axis, split_axis=split_dim, concat_axis=concat_dim,...]
    reduce_sum x3 -> x0, other arithmetic: 2.88 us -> none  [the longest x1 1.36 us: unit_rows(): scale = lax.rsqrt(jnp.sum(wide * wide, axis=-1, keepdims=True) + EPS)]
    all_to_all x2 -> x0, local copies, waits for them, and re-layouts: 1.61 us -> none  [sent_together(): lax.all_to_all(both, axis, split_axis=split_dim, concat_axis=concat_dim,...]
    dot_general x3 -> x0, matrix products: 1.49 us -> none  [the longest x1 0.86 us: per_device(): lax.dot_general(got_tags, got_rows, (((0,), (0,)), ((), ())), preferred_e...]
    unnamed x10 -> x2, local copies, waits for them, and re-layouts: 1.32 us -> 2.65 us
    convert_element_type x1 -> x0, other arithmetic: 1.33 us -> none  [unit_rows(): return (wide * scale).astype(jnp.bfloat16)]
    slice x0 -> x1, local copies, waits for them, and re-layouts: none -> 1.32 us  [per_device(): return (best.reshape(ROWS), sums, counts[:, 0])]
  transfers between devices with their start and end apart: 1 -> 0, of which waited for: 0 -> 0; matrix products, arithmetic and copies ran while one was open for 1% -> 0% of each run, Pallas kernels for 73% -> 0%
where the time goes in v2:
time: 80.6 us; the launch traced here: 80.4 us
  Pallas kernels  75.8 us (94%)
  local copies, waits for them, and re-layouts  3.98 us (5%)
    pallas_call x1, Pallas kernels, per_device(): pl.pallas_call(window_kernel, out_shape=(jax.ShapeDtypeStruct((1, ROWS),...  75.8 us
    unnamed x2, local copies, waits for them, and re-layouts  2.65 us

profile of v2, /device:TPU:1, one launch (start us, length us, event | category | flops | bytes accessed | tf_op | source)
XLA Modules:
  0.0 80.4 jit_solution(17275122837688613929)
XLA Ops:
  0.6 75.8 %shard_map.85 = (f32[1,512]{1,0:T(1,128)}, f32[16,768]{1,0:T(8,128)}, f32[16,128]{1,0:T(8,128)}) custom-call(bf16[512,768]{1,0:T(8,128)(2,1)} %new_hbm.1, bf16[4096,768]{1,0:T(8,128)(2,1)} %index_hbm.1, s32[8,128]{1,0:T(8,128)} %bitcast.6, s32[1,256]{1,0:T(1,128)} %bitcast.7, s32[1,256]{1,0:T(1,128)} %bitcast.8, s32[1,256]{1,0:T(1,128)} %bitcast.9), custom_call_target="tpu_custom_call" | custom-call | flops 25769803776 | bytes 10485760 | tf_op jit(solution)/shard_map/pallas_call | solution.py:347
  76.4 1.3 %slice_reduce_fusion = f32[16]{0:T(128)} fusion(f32[16,128]{1,0:T(8,128)} %get-tuple-element.8), kind=kLoop, calls=%fused_computation | loop fusion | bytes 128 | tf_op jit(solution)/shard_map/slice | solution.py:388
  77.7 1.2 %copy.11 = f32[512]{0:T(512)} copy(f32[512]{0:T(512)} %bitcast.5) | data formatting | bytes 4096
  79.0 1.4 %copy.12 = f32[16,768]{1,0:T(8,128)} copy(f32[16,768]{1,0:T(8,128)} %get-tuple-element.13) | data formatting | bytes 98304

commit v3 on v2

--- a/solution.py
+++ b/solution.py
@@ -45,18 +45,18 @@
     return [quad_at(4 + q % 2) + side + CH * (q // 2) for q in range(4)]
 
 
-CR_AT = (0, UC, 4 * UC, 5 * UC)
-XM_AT = (2 * UC, 6 * UC, 8 * UC, 10 * UC)
-XP_AT = (3 * UC, 7 * UC, 9 * UC, 11 * UC)
-X2_AT = (12 * UC, 13 * UC, 14 * UC, 15 * UC)
-AC_AT = (16 * UC, 16 * UC + CH)
-AY_AT = (16 * UC + 2 * CH, 16 * UC + 3 * CH)
+CR_AT = (0, UC, 2 * UC, 3 * UC)
+XM_AT = (384, 576, 1088, 768)
+XP_AT = (480, 672, 1184, 864)
+AC_AT = (960, 1280)
+X2_AT = (1408, 1504, 1600, 1696)
+AY_AT = (1792, 1920)
 
 
 def window_kernel(
-    new_hbm, index_hbm, pattern_hbm, row_hbm, owner_hbm, local_hbm, best_ref, sums_ref, counts_ref,
+    new_hbm, index_hbm, pattern_hbm, row_hbm, owner_hbm, local_hbm, best_ref, sums_ref,
     nr, ir, oi, acc0, acc1, ret_out, ret_in, pattern, kept, codes, weights, partial, got,
-    load_sem, z_s, z_r, z2_s, z2_r, sib_s, sib_r, cr_s, cr_r, ac_s, ac_r, ay_s, ay_r,
+    load_sem, z_s, z_r, z2_s, z2_r, sib_s, sib_r, cr_s, cr_r, yu_s, yu_r, ac_s, ac_r, ay_s, ay_r,
     x_s, x_r, x2_s, x2_r, ret_s, ret_r, code_s, code_r, sum_s, sum_r,
 ):
     b = lax.axis_index("blk")
@@ -75,7 +75,7 @@
     sib = (b, slab_of(0, 0, 1))
     cross = (blk_of(0, 1), slab_of(0, 1, 0))
     ylo = (b, slab_of(0, 1, 0))
-    back = [(dz, dc) for dz in (0, 1, 2, 3) for dc in (0, 1) if (dz, dc) != (0, 0)]
+    back = [(2, 0), (2, 1), (1, 0), (3, 0), (1, 1), (3, 1), (0, 1)]
     back_id = [(blk_of(dz), slab_of(0, 0, dc)) for dz, dc in back]
     plane = [(dh, dx, dl) for dx in (0, 1, 3, 2) for dh in (0, 1) for dl in (0, 1) if (dh, dx, dl) != (0, 0, 0)]
     plane_id = [(blk_of(0, dh), slab_of(dx, dl)) for dh, dx, dl in plane]
@@ -127,8 +127,9 @@
         remote(rows(nr, quad_at(k), 2 * CH), rows(nr, quad_at(k) + 2 * CH, 2 * CH), sib_s.at[k], sib_r.at[k], sib)
         for k in range(6)
     ]
-    unit_at = [pl.multiple_of(COMMON + x * UNIT + UC * k, 32) for k in range(4)]
-    cr = [remote(rows(ir, unit_at[k], UC), rows(oi, CR_AT[k], UC), cr_s.at[k], cr_r.at[k], cross) for k in range(4)]
+    unit_at = [pl.multiple_of(COMMON + x * UNIT + UC * k, 32) for k in (3 * (1 - l), 1, 2, 3 * l)]
+    cr = [remote(rows(ir, unit_at[k], UC), rows(oi, CR_AT[k], UC), cr_s.at[k], cr_r.at[k], cross) for k in range(3)]
+    yu = [remote(rows(oi, CR_AT[0], UC), rows(oi, CR_AT[3], UC), yu_s.at[0], yu_r.at[0], ylo)]
     common_at = [pl.multiple_of(half_to + CH * k, CH) for k in range(2)]
     ac = [remote(rows(ir, common_at[k]), rows(oi, AC_AT[k]), ac_s.at[k], ac_r.at[k], cross) for k in range(2)]
     ay = [remote(rows(oi, AC_AT[k]), rows(oi, AY_AT[k]), ay_s.at[k], ay_r.at[k], ylo) for k in range(2)]
@@ -169,13 +170,14 @@
         cp.wait()
     codes[0] = (kept[1] * CL_DEV + kept[2]) * ROWS + kept[0]
     pl.semaphore_wait(barrier, len(partners))
+    for cp in code:
+        cp.start()
     for k in range(4):
         own_p[k].start()
         own_m[k].start()
-        cr[k].start()
+    for cp in cr:
+        cp.start()
     to_sib[0].start()
-    for cp in code:
-        cp.start()
     loads[2].wait()
     for k in range(2):
         normalize(ir, common_at[k])
@@ -214,7 +216,9 @@
         pair_sib[k].start()
 
     def cross_in(k):
-        cr[k].wait_recv()
+        (cr + yu)[k].wait_recv()
+        if k == 0:
+            yu[0].start()
         x_p[k].start()
         x_m[k].start()
 
@@ -262,63 +266,64 @@
         partial[:, pl.ds(0, D)] = part if first else partial[:, pl.ds(0, D)] + part
 
     own_range(0)
+    count = weigh(0, 0, 0)
     to_sib[0].wait_recv()
     own_range(ROWS)
     cross_in(0)
-    z_in(0)
-    count = weigh(0, 0, 0)
     for i, (dz, dc) in enumerate(back):
         code[i].wait_recv()
         count = count + weigh(1 + i, (4 - dz) % 4, dc)
         if i == 3:
-            cross_in(1)
+            z_in(0)
     partial[:, pl.ds(D, 128)] = jnp.broadcast_to(count, (PLANE, 128))
+    cross_in(1)
     quad(0)
+    cross_in(3)
     x_in(0)
     z_in(1)
     cross_in(2)
     quad(1)
     x_in(1)
-    cross_in(3)
-    other_range(0, 4 * UC, 0, 2048)
+    other_range(0, 768, 512, 2048)
     z_in(2)
     quad(2)
+    other_range(0, 768, 2048, 2560)
+    common_in(0)
+    x_in(3)
+    z_in(3)
+    other_range(768, 1088, 512, 2560)
+    quad(3)
     x_in(2)
-    other_range(4 * UC, 8 * UC, 0, 2048)
-    z_in(3)
-    common_in(0)
-    quad(3)
-    x_in(3)
-    other_range(0, 8 * UC, 2048, 3072)
     common_in(1)
-    other_range(8 * UC, 12 * UC, 0, 3072)
+    other_range(0, 1088, 2560, 3072)
+    z_in(4)
+    other_range(1088, 1408, 512, 3072)
+    quad(4)
     add_rows(0, 3072, True)
-    z_in(4)
-    quad(4)
-    for k in range(4):
-        x_f[k].wait_recv()
-    other_range(12 * UC, 16 * UC + 2 * CH, 0, 3072)
+    other_range(0, 1408, 3072, 3584)
     z_in(5)
     pair_sib[5].wait_recv()
     add_rows(3072, 4096, False)
     for cp in sums:
         cp.start()
     own_range(quad_at(5))
-    other_range(0, 16 * UC + 2 * CH, 3072, 4096)
+    for k in range(4):
+        x_f[k].wait_recv()
     for cp in ay:
         cp.wait_recv()
-    other_range(16 * UC + 2 * CH, HALF, 0, 4096)
+    other_range(1408, HALF, 512, 3584)
+    other_range(0, HALF, 3584, 4096)
 
     def block_best(dz, dc):
         row = blk_of(dz) * 16 + slab_of(0, 0, dc)
-        live0 = jnp.full((1, ROWS), pattern[b, row], jnp.int32) > 0
-        live1 = jnp.full((1, ROWS), pattern[blk_of(0, 1), row], jnp.int32) > 0
-
-        def top(acc):
-            parts = [jnp.max(acc[:, pl.ds(w, CH)], axis=0, keepdims=True) for w in places(dz, dc)]
-            return jnp.concatenate(parts, axis=1)
-
-        return jnp.maximum(jnp.where(live0, top(acc0), -2.0), jnp.where(live1, top(acc1), -2.0))
+        live0 = jnp.full((8, CH), pattern[b, row], jnp.int32) > 0
+        live1 = jnp.full((8, CH), pattern[blk_of(0, 1), row], jnp.int32) > 0
+        parts = []
+        for w in places(dz, dc):
+            here = jnp.where(live0, acc0[:, pl.ds(w, CH)], -2.0)
+            there = jnp.where(live1, acc1[:, pl.ds(w, CH)], -2.0)
+            parts.append(jnp.max(jnp.maximum(here, there), axis=0, keepdims=True))
+        return jnp.concatenate(parts, axis=1)
 
     rets = []
     for i, (dz, dc) in enumerate(back):
@@ -326,33 +331,40 @@
         cp = remote(ret_out.at[i], ret_in.at[i], ret_s.at[i], ret_r.at[i], back_id[i])
         cp.start()
         rets.append(cp)
+    other_range(0, HALF, 0, 512)
     best = block_best(0, 0)
     total = partial[cluster_rows(0, 0, 0), :]
     for j, cp in enumerate(sums):
         cp.wait_recv()
         total = total + got[j]
-    sums_ref[...] = total[:, :D]
-    counts_ref[...] = total[:, D:]
+    sums_ref[...] = total
     for i, cp in enumerate(rets):
         cp.wait_recv()
         best = jnp.maximum(best, ret_in[i])
     best_ref[...] = best
-    for cp in own_p + own_m + fwd_p + fwd_m + to_sib + pair_sib + cr + ac + ay + x_p + x_m + x_f + code + sums + rets:
+    for cp in own_p + own_m + fwd_p + fwd_m + to_sib + pair_sib + cr + yu + ac + ay + x_p + x_m + x_f + code + sums + rets:
         cp.wait_send()
+
+
+def parted(best_in, sums_in, best_ref, sums_ref, counts_ref):
+    best_ref[...] = best_in[...]
+    sums_ref[...] = sums_in[:, :D]
+    counts = sums_in[:, D:]
+    at = [lax.broadcasted_iota(jnp.int32, counts.shape, axis) for axis in (0, 1)]
+    counts_ref[...] = jnp.sum(jnp.where(at[0] == at[1], counts, 0.0), axis=0, keepdims=True)[:, :CL_DEV]
 
 
 def per_device(new_rows, index_rows, pattern, kept_row, kept_owner, kept_local):
     dma = pltpu.SemaphoreType.DMA
     f32, bf16, i32 = jnp.float32, jnp.bfloat16, jnp.int32
-    best, sums, counts = pl.pallas_call(
+    best, sums = pl.pallas_call(
         window_kernel,
         out_shape=(
             jax.ShapeDtypeStruct((1, ROWS), f32),
-            jax.ShapeDtypeStruct((CL_DEV, D), f32),
-            jax.ShapeDtypeStruct((CL_DEV, 128), f32),
+            jax.ShapeDtypeStruct((CL_DEV, WIDE), f32),
         ),
         in_specs=[pl.BlockSpec(memory_space=pl.ANY)] * 6,
-        out_specs=[pl.BlockSpec(memory_space=pltpu.VMEM)] * 3,
+        out_specs=[pl.BlockSpec(memory_space=pltpu.VMEM)] * 2,
         scratch_shapes=[
             pltpu.VMEM((8 * ROWS, D), bf16),
             pltpu.VMEM((HALF, D), bf16),
@@ -369,7 +381,7 @@
             pltpu.VMEM((15, CL_DEV, WIDE), f32),
             dma((11,)),
             dma((2, 4)), dma((2, 4)), dma((2, 2)), dma((2, 2)), dma((7,)), dma((7,)), dma((4,)), dma((4,)),
-            dma((2,)), dma((2,)), dma((2,)), dma((2,)),
+            dma((1,)), dma((1,)), dma((2,)), dma((2,)), dma((2,)), dma((2,)),
             dma((2, 4)), dma((2, 4)), dma((4,)), dma((4,)), dma((7,)), dma((7,)), dma((7,)), dma((7,)),
             dma((15,)), dma((15,)),
         ],
@@ -385,7 +397,17 @@
         kept_owner.reshape(1, KEEP),
         kept_local.reshape(1, KEEP),
     )
-    return (best.reshape(ROWS), sums, counts[:, 0])
+    best, sums, counts = pl.pallas_call(
+        parted,
+        out_shape=(
+            jax.ShapeDtypeStruct((1, ROWS), f32),
+            jax.ShapeDtypeStruct((CL_DEV, D), f32),
+            jax.ShapeDtypeStruct((1, CL_DEV), f32),
+        ),
+        in_specs=[pl.BlockSpec(memory_space=pltpu.VMEM)] * 2,
+        out_specs=[pl.BlockSpec(memory_space=pltpu.VMEM)] * 3,
+    )(best, sums)
+    return (best.reshape(ROWS), sums, counts.reshape(CL_DEV))
 
 
 def solution(mesh):

time: 80.6 us -> 60.9 us (0.76)
  Pallas kernels: 75.8 us -> 60.1 us
  local copies, waits for them, and re-layouts: 3.98 us -> 0 us
    pallas_call x1, Pallas kernels: 75.8 us -> 58.6 us  [per_device(): pl.pallas_call(window_kernel, out_shape=(jax.ShapeDtypeStruct((1, ROWS),...]
    unnamed x2 -> x0, local copies, waits for them, and re-layouts: 2.65 us -> none
    pallas_call x0 -> x1, Pallas kernels: none -> 1.45 us  [per_device(): pl.pallas_call(parted, out_shape=(jax.ShapeDtypeStruct((1, ROWS), f32), j...]
    slice x1 -> x0, local copies, waits for them, and re-layouts: 1.32 us -> none  [per_device(): return (best.reshape(ROWS), sums, counts[:, 0])]
where the time goes in v3:
time: 60.9 us; the launch traced here: 60.7 us
  Pallas kernels  60.1 us (99%)
  between operations  0.64 us (1%)
    pallas_call x1, Pallas kernels, per_device(): pl.pallas_call(window_kernel, out_shape=(jax.ShapeDtypeStruct((1, ROWS),...  58.6 us
    pallas_call x1, Pallas kernels, per_device(): pl.pallas_call(parted, out_shape=(jax.ShapeDtypeStruct((1, ROWS), f32), j...  1.45 us

profile of v3, /device:TPU:1, one launch (start us, length us, event | category | flops | bytes accessed | tf_op | source)
XLA Modules:
  0.0 60.7 jit_solution(9358015633220105630)
XLA Ops:
  0.6 58.6 %shard_map.85 = (f32[1,512]{1,0:T(1,128)}, f32[16,896]{1,0:T(8,128)}) custom-call(bf16[512,768]{1,0:T(8,128)(2,1)} %new_hbm.1, bf16[4096,768]{1,0:T(8,128)(2,1)} %index_hbm.1, s32[8,128]{1,0:T(8,128)} %bitcast.6, s32[1,256]{1,0:T(1,128)} %bitcast.8, s32[1,256]{1,0:T(1,128)} %bitcast.9, s32[1,256]{1,0:T(1,128)} %bitcast.10), custom_call_target="tpu_custom_call" | custom-call | flops 25769803776 | bytes 10485760 | tf_op jit(solution)/shard_map/pallas_call | solution.py:360
  59.3 1.4 %shard_map.86 = (f32[1,512]{1,0:T(1,128)}, f32[16,768]{1,0:T(8,128)}, f32[1,16]{1,0:T(1,128)}) custom-call(f32[1,512]{1,0:T(1,128)} %get-tuple-element.8.best_in, f32[16,896]{1,0:T(8,128)} %get-tuple-element.9.sums_in), custom_call_target="tpu_custom_call" | custom-call | tf_op jit(solution)/shard_map/pallas_call | solution.py:400

commit v4 on v3

--- a/solution.py
+++ b/solution.py
@@ -13,10 +13,12 @@
 CH = 128
 D = 768
 HALF = 2048
-UC = 96
+UC = 80
 UNIT = 4 * UC
-COMMON = 512
+COMMON = 768
 WIDE = D + 128
+KCAP = 4
+LATE = 3072
 PLANE = 256
 
 
@@ -46,18 +48,19 @@
 
 
 CR_AT = (0, UC, 2 * UC, 3 * UC)
-XM_AT = (384, 576, 1088, 768)
-XP_AT = (480, 672, 1184, 864)
-AC_AT = (960, 1280)
-X2_AT = (1408, 1504, 1600, 1696)
-AY_AT = (1792, 1920)
+XM_AT = (320, 480, 928, 640)
+XP_AT = (400, 560, 1008, 720)
+AC_AT = (800, 1088, 1536)
+X2_AT = (1216, 1296, 1376, 1456)
+AY_AT = (1664, 1792, 1920)
 
 
 def window_kernel(
-    new_hbm, index_hbm, pattern_hbm, row_hbm, owner_hbm, local_hbm, best_ref, sums_ref,
+    new_hbm, index_hbm, pattern_hbm, row_hbm, owner_hbm, local_hbm, best_ref, sums_ref, counts_ref,
     nr, ir, oi, acc0, acc1, ret_out, ret_in, pattern, kept, codes, weights, partial, got,
+    late_weights, late, late_got, tags, tally,
     load_sem, z_s, z_r, z2_s, z2_r, sib_s, sib_r, cr_s, cr_r, yu_s, yu_r, ac_s, ac_r, ay_s, ay_r,
-    x_s, x_r, x2_s, x2_r, ret_s, ret_r, code_s, code_r, sum_s, sum_r,
+    x_s, x_r, x2_s, x2_r, ret_s, ret_r, code_s, code_r, sum_s, sum_r, late_s, late_r,
 ):
     b = lax.axis_index("blk")
     s = lax.axis_index("slab")
@@ -91,12 +94,12 @@
     loads = [pltpu.make_async_copy(new_hbm, rows(nr, 0, ROWS), load_sem.at[0])]
     half_to = pl.multiple_of((1 - l) * (COMMON // 2), 128)
     half_here = pl.multiple_of(l * (COMMON // 2), 128)
-    index_parts = [(pl.multiple_of(COMMON + x * UNIT, 128), UNIT), (half_to, COMMON // 2), (half_here, COMMON // 2)]
-    index_parts += [(pl.multiple_of(COMMON + ring4(x + j) * UNIT, 128), UNIT) for j in (1, 2, 3)]
+    index_parts = [(pl.multiple_of(COMMON + x * UNIT, 64), UNIT), (half_to, COMMON // 2), (half_here, COMMON // 2)]
+    index_parts += [(pl.multiple_of(COMMON + ring4(x + j) * UNIT, 64), UNIT) for j in (1, 2, 3)]
     for j, (at, n) in enumerate(index_parts):
         loads.append(
             pltpu.make_async_copy(
-                index_hbm.at[pl.ds(pl.multiple_of(c * HALF + at, 128), n)], rows(ir, at, n), load_sem.at[1 + j]
+                index_hbm.at[pl.ds(pl.multiple_of(c * HALF + at, 64), n)], rows(ir, at, n), load_sem.at[1 + j]
             )
         )
     small = [
@@ -127,12 +130,12 @@
         remote(rows(nr, quad_at(k), 2 * CH), rows(nr, quad_at(k) + 2 * CH, 2 * CH), sib_s.at[k], sib_r.at[k], sib)
         for k in range(6)
     ]
-    unit_at = [pl.multiple_of(COMMON + x * UNIT + UC * k, 32) for k in (3 * (1 - l), 1, 2, 3 * l)]
+    unit_at = [pl.multiple_of(COMMON + x * UNIT + UC * k, 16) for k in (3 * (1 - l), 1, 2, 3 * l)]
     cr = [remote(rows(ir, unit_at[k], UC), rows(oi, CR_AT[k], UC), cr_s.at[k], cr_r.at[k], cross) for k in range(3)]
     yu = [remote(rows(oi, CR_AT[0], UC), rows(oi, CR_AT[3], UC), yu_s.at[0], yu_r.at[0], ylo)]
-    common_at = [pl.multiple_of(half_to + CH * k, CH) for k in range(2)]
-    ac = [remote(rows(ir, common_at[k]), rows(oi, AC_AT[k]), ac_s.at[k], ac_r.at[k], cross) for k in range(2)]
-    ay = [remote(rows(oi, AC_AT[k]), rows(oi, AY_AT[k]), ay_s.at[k], ay_r.at[k], ylo) for k in range(2)]
+    common_at = [pl.multiple_of(half_to + CH * k, CH) for k in range(3)]
+    ac = [remote(rows(ir, common_at[k]), rows(oi, AC_AT[k]), ac_s.at[k], ac_r.at[k], cross) for k in range(3)]
+    ay = [remote(rows(oi, AC_AT[k]), rows(oi, AY_AT[k]), ay_s.at[k], ay_r.at[k], ylo) for k in range(3)]
     x_p = [remote(rows(oi, CR_AT[k], UC), rows(oi, XM_AT[k], UC), x_s.at[0, k], x_r.at[0, k], xp) for k in range(4)]
     x_m = [remote(rows(oi, CR_AT[k], UC), rows(oi, XP_AT[k], UC), x_s.at[1, k], x_r.at[1, k], xm) for k in range(4)]
     x_f = [
@@ -149,6 +152,11 @@
 
     sums = [
         remote(partial.at[cluster_rows(*plane[j])], got.at[j], sum_s.at[j], sum_r.at[j], plane_id[j])
+        for j in range(len(plane))
+    ]
+
+    lates = [
+        remote(late.at[place_of(*plane[j])], late_got.at[j], late_s.at[j], late_r.at[j], plane_id[j])
         for j in range(len(plane))
     ]
 
@@ -169,25 +177,9 @@
     for cp in small:
         cp.wait()
     codes[0] = (kept[1] * CL_DEV + kept[2]) * ROWS + kept[0]
-    pl.semaphore_wait(barrier, len(partners))
-    for cp in code:
-        cp.start()
-    for k in range(4):
-        own_p[k].start()
-        own_m[k].start()
-    for cp in cr:
-        cp.start()
-    to_sib[0].start()
     loads[2].wait()
-    for k in range(2):
+    for k in range(3):
         normalize(ir, common_at[k])
-        ac[k].start()
-    for j in range(2, 6):
-        loads[1 + j].wait()
-        at, n = index_parts[j]
-        for k in range(n // CH):
-            normalize(ir, pl.multiple_of(at + CH * k, CH))
-
     def scores(acc, idx, i_at, i_n, n_at, n_n):
         prod = lax.dot_general(
             idx[pl.ds(i_at, i_n), :], nr[pl.ds(n_at, n_n), :],
@@ -196,24 +188,16 @@
         top = jnp.max(prod.reshape(i_n // 8, 8, n_n), axis=0)
         acc[:, pl.ds(n_at, n_n)] = jnp.maximum(acc[:, pl.ds(n_at, n_n)], top)
 
-    def own_range(n_at):
-        scores(acc0, ir, 0, HALF, n_at, ROWS)
+    def own_range(n_at, n_end):
+        scores(acc0, ir, 0, HALF, n_at, n_end - n_at)
 
     def other_range(i_at, i_end, n_at, n_end):
         scores(acc1, oi, i_at, i_end - i_at, n_at, n_end - n_at)
 
-    def z_in(k):
-        if k < 4:
-            own_p[k].wait_recv()
-            if k < 2:
-                fwd_p[k].start()
-            own_m[k].wait_recv()
-            if k < 2:
-                fwd_m[k].start()
-        else:
-            fwd_p[k - 4].wait_recv()
-            fwd_m[k - 4].wait_recv()
-        pair_sib[k].start()
+    def z_in(k, side):
+        (own_p, own_m)[side][k].wait_recv()
+        if k < 2:
+            (fwd_p, fwd_m)[side][k].start()
 
     def cross_in(k):
         (cr + yu)[k].wait_recv()
@@ -226,17 +210,17 @@
         ac[k].wait_recv()
         ay[k].start()
 
-    def x_in(k):
-        x_p[k].wait_recv()
-        if k % 2 == 0:
+    def x_in(k, side):
+        (x_p, x_m)[side][k].wait_recv()
+        if k % 2 == side:
             x_f[k].start()
-        x_m[k].wait_recv()
-        if k % 2 == 1:
-            x_f[k].start()
-
-    def quad(k):
-        pair_sib[k].wait_recv()
-        own_range(quad_at(k))
+
+    def hot(count, which):
+        at = lax.broadcasted_iota(jnp.int32, (count, KEEP), 0)
+        return jnp.where(at == which, 1.0, 0.0).astype(jnp.bfloat16)
+
+    def product(left, right):
+        return lax.dot_general(left, right, (((1,), (1,)), ((), ())), preferred_element_type=jnp.float32)
 
     def weigh(slot, dz, dc):
         both = codes[slot]
@@ -245,74 +229,151 @@
         owner = lax.div(both, ROWS * CL_DEV)
         o_blk, o_slab = lax.div(owner, 16), lax.rem(owner, 16)
         mine = (lax.div(o_blk, 2) == z) & (lax.rem(o_slab, 2) == c)
-        cluster = (lax.rem(o_blk, 2) * 8 + lax.div(o_slab, 2)) * CL_DEV + local
-        cluster = jnp.where(mine, cluster, -1)
-
-        def hot(count, which):
-            at = lax.broadcasted_iota(jnp.int32, (count, KEEP), 0)
-            return jnp.where(at == which, 1.0, 0.0).astype(jnp.bfloat16)
-
-        named = lax.dot_general(
-            hot(PLANE, cluster), hot(ROWS, row), (((1,), (1,)), ((), ())), preferred_element_type=jnp.float32
-        )
+        place = jnp.where(mine, lax.rem(o_blk, 2) * 8 + lax.div(o_slab, 2), -1)
+        named = hot(PLANE, jnp.where(mine, place * CL_DEV + local, -1))
+        count = jnp.sum(named.astype(jnp.float32), axis=1, keepdims=True)
+        if dz != 2:
+            table, width, first = weights, named, 0
+        else:
+            to = hot(16, place)
+            before, after = (lax.broadcasted_iota(jnp.int32, (KEEP, KEEP), axis) for axis in (0, 1))
+            sooner = jnp.where(before < after, 1.0, 0.0).astype(jnp.bfloat16)
+            sooner = jnp.dot(to, sooner, preferred_element_type=jnp.float32)
+            rank = jnp.sum(to.astype(jnp.float32) * sooner, axis=0, keepdims=True).astype(jnp.int32)
+            table, first = late_weights, LATE
+            width = hot(8 * 16, jnp.where(mine, place * 8 + dc * KCAP + rank, -1))
+        spread = product(width, hot(ROWS, row)).astype(jnp.bfloat16)
         for q, at in enumerate(places(dz, dc)):
-            weights[:, pl.ds(at, CH)] = named[:, CH * q : CH * (q + 1)].astype(jnp.bfloat16)
-        return jnp.sum(named, axis=1, keepdims=True)
-
-    def add_rows(n_at, n_end, first):
-        part = jnp.dot(
-            weights[:, pl.ds(n_at, n_end - n_at)], nr[pl.ds(n_at, n_end - n_at), :], preferred_element_type=jnp.float32
-        )
-        partial[:, pl.ds(0, D)] = part if first else partial[:, pl.ds(0, D)] + part
-
-    own_range(0)
-    count = weigh(0, 0, 0)
+            table[:, pl.ds(at - first, CH)] = spread[:, CH * q : CH * (q + 1)]
+        return count, product(width, hot(128, local)) if dz == 2 else 0.0
+
+    def send_sums():
+        partial[...] = jnp.dot(weights[...], nr[pl.ds(0, LATE), :], preferred_element_type=jnp.float32)
+        for cp in sums:
+            cp.start()
+
+    def send_late():
+        picked = jnp.dot(late_weights[...], nr[pl.ds(LATE, 2 * ROWS), :], preferred_element_type=jnp.float32)
+        for q in range(16):
+            late[q, :, pl.ds(0, D)] = picked[8 * q : 8 * (q + 1)].astype(jnp.bfloat16)
+        late_got[15] = late[place_of(0, 0, 0)]
+        for cp in lates:
+            cp.start()
+
+    def weigh_next(i):
+        dz, dc = back[i]
+        code[i].wait_recv()
+        more, tag = weigh(1 + i, (4 - dz) % 4, dc)
+        tally[...] = tally[...] + more
+        if dz == 2:
+            tags[...] = tags[...] + tag
+
+    def write_tags():
+        lane = lax.broadcasted_iota(jnp.int32, (8, 128), 1)
+        for q in range(16):
+            mixed = tags[pl.ds(8 * q, 8), :]
+            for g in range(2):
+                mixed = jnp.where(lane == CL_DEV + g, tally[pl.ds(16 * q + 8 * g, 8), :], mixed)
+            late[q, :, pl.ds(D, 128)] = mixed.astype(jnp.bfloat16)
+
+    for j in range(2, 6):
+        loads[1 + j].wait()
+        at, n = index_parts[j]
+        step = CH if n % CH == 0 else UC
+        for k in range(n // step):
+            normalize(ir, pl.multiple_of(at + step * k, 16), step)
+
+    pl.semaphore_wait(barrier, len(partners))
+    for cp in code:
+        cp.start()
+    for k in range(4):
+        own_p[k].start()
+        own_m[k].start()
+    for cp in cr + ac:
+        cp.start()
+    to_sib[0].start()
+    own_range(0, ROWS)
+    count, _ = weigh(0, 0, 0)
+    tally[...] = jnp.broadcast_to(count, (PLANE, 128))
+    tags[...] = jnp.zeros(tags.shape, jnp.float32)
+    weigh_next(0)
+    weigh_next(1)
+    weigh_next(2)
+    weigh_next(3)
+    weigh_next(4)
+    weigh_next(5)
     to_sib[0].wait_recv()
-    own_range(ROWS)
+    own_range(512, 1024)
+    weigh_next(6)
+    write_tags()
     cross_in(0)
-    for i, (dz, dc) in enumerate(back):
-        code[i].wait_recv()
-        count = count + weigh(1 + i, (4 - dz) % 4, dc)
-        if i == 3:
-            z_in(0)
-    partial[:, pl.ds(D, 128)] = jnp.broadcast_to(count, (PLANE, 128))
+    z_in(0, 0)
+    z_in(0, 1)
+    pair_sib[0].start()
+    own_range(1024, 1280)
     cross_in(1)
-    quad(0)
+    pair_sib[0].wait_recv()
+    own_range(1280, 1536)
     cross_in(3)
-    x_in(0)
-    z_in(1)
+    x_in(0, 0)
+    x_in(0, 1)
     cross_in(2)
-    quad(1)
-    x_in(1)
-    other_range(0, 768, 512, 2048)
-    z_in(2)
-    quad(2)
-    other_range(0, 768, 2048, 2560)
+    other_range(0, 480, 512, 1536)
+    z_in(1, 0)
+    z_in(1, 1)
+    pair_sib[1].start()
+    own_range(1536, 1792)
+    x_in(1, 0)
+    x_in(1, 1)
+    pair_sib[1].wait_recv()
+    own_range(1792, 2048)
     common_in(0)
-    x_in(3)
-    z_in(3)
-    other_range(768, 1088, 512, 2560)
-    quad(3)
-    x_in(2)
+    z_in(2, 0)
+    z_in(2, 1)
+    pair_sib[2].start()
+    x_in(3, 0)
+    x_in(3, 1)
+    other_range(0, 928, 1536, 2304)
+    other_range(480, 928, 512, 1536)
+    pair_sib[2].wait_recv()
+    own_range(2048, 2560)
+    x_f[0].wait_recv()
+    x_in(2, 1)
     common_in(1)
-    other_range(0, 1088, 2560, 3072)
-    z_in(4)
-    other_range(1088, 1408, 512, 3072)
-    quad(4)
-    add_rows(0, 3072, True)
-    other_range(0, 1408, 3072, 3584)
-    z_in(5)
+    z_in(3, 0)
+    z_in(3, 1)
+    pair_sib[3].start()
+    other_range(1008, 1296, 512, 2816)
+    x_in(2, 0)
+    x_f[1].wait_recv()
+    ay[0].wait_recv()
+    other_range(0, 928, 2304, 2816)
+    pair_sib[3].wait_recv()
+    own_range(2560, 3072)
+    common_in(2)
+    x_f[3].wait_recv()
+    fwd_p[0].wait_recv()
+    fwd_m[0].wait_recv()
+    pair_sib[4].start()
+    other_range(0, 1296, 2816, 3328)
+    other_range(1456, 1792, 512, 3328)
+    x_f[2].wait_recv()
+    pair_sib[4].wait_recv()
+    ay[1].wait_recv()
+    send_sums()
+    fwd_p[1].wait_recv()
+    fwd_m[1].wait_recv()
+    pair_sib[5].start()
+    own_range(3072, 3584)
     pair_sib[5].wait_recv()
-    add_rows(3072, 4096, False)
-    for cp in sums:
-        cp.start()
-    own_range(quad_at(5))
-    for k in range(4):
-        x_f[k].wait_recv()
-    for cp in ay:
-        cp.wait_recv()
-    other_range(1408, HALF, 512, 3584)
-    other_range(0, HALF, 3584, 4096)
+    send_late()
+    ay[2].wait_recv()
+    other_range(0, 2048, 3328, 3840)
+    own_range(3584, 4096)
+    other_range(1792, 2048, 512, 3328)
+    other_range(0, 2048, 3840, 4096)
+    other_range(1296, 1456, 512, 3328)
+    other_range(928, 1008, 512, 2816)
 
     def block_best(dz, dc):
         row = blk_of(dz) * 16 + slab_of(0, 0, dc)
@@ -337,34 +398,44 @@
     for j, cp in enumerate(sums):
         cp.wait_recv()
         total = total + got[j]
-    sums_ref[...] = total
+    for cp in lates:
+        cp.wait_recv()
+    slots = late_got[...].astype(jnp.float32).reshape(16 * 8, WIDE)
+    clusters = slots[:, D:].T.astype(jnp.bfloat16)
+    last = jnp.dot(clusters, slots[:, :D].astype(jnp.bfloat16), preferred_element_type=jnp.float32)
+    sums_ref[...] = total + last[:CL_DEV]
+    counts_ref[...] = jnp.sum(late_got[:, :, pl.ds(D, 128)].astype(jnp.float32), axis=0)
     for i, cp in enumerate(rets):
         cp.wait_recv()
         best = jnp.maximum(best, ret_in[i])
     best_ref[...] = best
-    for cp in own_p + own_m + fwd_p + fwd_m + to_sib + pair_sib + cr + yu + ac + ay + x_p + x_m + x_f + code + sums + rets:
+    for cp in own_p + own_m + fwd_p + fwd_m + to_sib + pair_sib + cr + yu + ac + ay + x_p + x_m + x_f + code + sums + lates + rets:
         cp.wait_send()
 
 
-def parted(best_in, sums_in, best_ref, sums_ref, counts_ref):
+def parted(best_in, sums_in, counts_in, best_ref, sums_ref, counts_ref):
     best_ref[...] = best_in[...]
-    sums_ref[...] = sums_in[:, :D]
-    counts = sums_in[:, D:]
-    at = [lax.broadcasted_iota(jnp.int32, counts.shape, axis) for axis in (0, 1)]
-    counts_ref[...] = jnp.sum(jnp.where(at[0] == at[1], counts, 0.0), axis=0, keepdims=True)[:, :CL_DEV]
+    sums_ref[...] = sums_in[...]
+    row, lane = (lax.broadcasted_iota(jnp.int32, (8, 128), axis) for axis in (0, 1))
+    counts = 0.0
+    for g in range(2):
+        column = counts_in[:, CL_DEV + g : CL_DEV + g + 1]
+        counts = counts + jnp.where(lane == row + 8 * g, column, 0.0)
+    counts_ref[...] = jnp.sum(counts, axis=0, keepdims=True)[:, :CL_DEV]
 
 
 def per_device(new_rows, index_rows, pattern, kept_row, kept_owner, kept_local):
     dma = pltpu.SemaphoreType.DMA
     f32, bf16, i32 = jnp.float32, jnp.bfloat16, jnp.int32
-    best, sums = pl.pallas_call(
+    best, sums, counts = pl.pallas_call(
         window_kernel,
         out_shape=(
             jax.ShapeDtypeStruct((1, ROWS), f32),
-            jax.ShapeDtypeStruct((CL_DEV, WIDE), f32),
+            jax.ShapeDtypeStruct((CL_DEV, D), f32),
+            jax.ShapeDtypeStruct((8, 128), f32),
         ),
         in_specs=[pl.BlockSpec(memory_space=pl.ANY)] * 6,
-        out_specs=[pl.BlockSpec(memory_space=pltpu.VMEM)] * 2,
+        out_specs=[pl.BlockSpec(memory_space=pltpu.VMEM)] * 3,
         scratch_shapes=[
             pltpu.VMEM((8 * ROWS, D), bf16),
             pltpu.VMEM((HALF, D), bf16),
@@ -376,14 +447,19 @@
             pltpu.SMEM((8, 128), i32),
             pltpu.VMEM((3, 1, KEEP), i32),
             pltpu.VMEM((8, 1, KEEP), i32),
-            pltpu.VMEM((PLANE, 8 * ROWS), bf16),
-            pltpu.VMEM((PLANE, WIDE), f32),
-            pltpu.VMEM((15, CL_DEV, WIDE), f32),
+            pltpu.VMEM((PLANE, LATE), bf16),
+            pltpu.VMEM((PLANE, D), f32),
+            pltpu.VMEM((15, CL_DEV, D), f32),
+            pltpu.VMEM((8 * 16, 2 * ROWS), bf16),
+            pltpu.VMEM((16, 8, WIDE), bf16),
+            pltpu.VMEM((16, 8, WIDE), bf16),
+            pltpu.VMEM((8 * 16, 128), f32),
+            pltpu.VMEM((PLANE, 128), f32),
             dma((11,)),
             dma((2, 4)), dma((2, 4)), dma((2, 2)), dma((2, 2)), dma((7,)), dma((7,)), dma((4,)), dma((4,)),
-            dma((1,)), dma((1,)), dma((2,)), dma((2,)), dma((2,)), dma((2,)),
+            dma((1,)), dma((1,)), dma((3,)), dma((3,)), dma((3,)), dma((3,)),
             dma((2, 4)), dma((2, 4)), dma((4,)), dma((4,)), dma((7,)), dma((7,)), dma((7,)), dma((7,)),
-            dma((15,)), dma((15,)),
+            dma((15,)), dma((15,)), dma((15,)), dma((15,)),
         ],
         compiler_params=pltpu.CompilerParams(
             collective_id=0, has_side_effects=True, vmem_limit_bytes=56 << 20
@@ -404,9 +480,9 @@
             jax.ShapeDtypeStruct((CL_DEV, D), f32),
             jax.ShapeDtypeStruct((1, CL_DEV), f32),
         ),
-        in_specs=[pl.BlockSpec(memory_space=pltpu.VMEM)] * 2,
+        in_specs=[pl.BlockSpec(memory_space=pltpu.VMEM)] * 3,
         out_specs=[pl.BlockSpec(memory_space=pltpu.VMEM)] * 3,
-    )(best, sums)
+    )(best, sums, counts)
     return (best.reshape(ROWS), sums, counts.reshape(CL_DEV))
 
 

time: 60.9 us -> 57.9 us (0.951)
  Pallas kernels: 60.1 us -> 56.9 us
    pallas_call x1, Pallas kernels: 58.6 us -> 55.5 us  [per_device(): pl.pallas_call(window_kernel, out_shape=(jax.ShapeDtypeStruct((1, ROWS),...]
where the time goes in v4:
time: 57.9 us; the launch traced here: 57.6 us
  Pallas kernels  56.9 us (98%)
  between operations  0.64 us (1%)
    pallas_call x1, Pallas kernels, per_device(): pl.pallas_call(window_kernel, out_shape=(jax.ShapeDtypeStruct((1, ROWS),...  55.5 us
    pallas_call x1, Pallas kernels, per_device(): pl.pallas_call(parted, out_shape=(jax.ShapeDtypeStruct((1, ROWS), f32), j...  1.43 us

profile of v4, /device:TPU:1, one launch (start us, length us, event | category | flops | bytes accessed | tf_op | source)
XLA Modules:
  0.0 57.6 jit_solution(11040625877559894228)
XLA Ops:
  0.6 55.5 %shard_map.85 = (f32[1,512]{1,0:T(1,128)}, f32[16,768]{1,0:T(8,128)}, f32[8,128]{1,0:T(8,128)}) custom-call(bf16[512,768]{1,0:T(8,128)(2,1)} %new_hbm.1, bf16[4096,768]{1,0:T(8,128)(2,1)} %index_hbm.1, s32[8,128]{1,0:T(8,128)} %bitcast.6, s32[1,256]{1,0:T(1,128)} %bitcast.8, s32[1,256]{1,0:T(1,128)} %bitcast.9, s32[1,256]{1,0:T(1,128)} %bitcast.10), custom_call_target="tpu_custom_call" | custom-call | flops 25769803776 | bytes 10485760 | tf_op jit(solution)/shard_map/pallas_call | solution.py:430
  56.2 1.4 %shard_map.86 = (f32[1,512]{1,0:T(1,128)}, f32[16,768]{1,0:T(8,128)}, f32[1,16]{1,0:T(1,128)}) custom-call(f32[1,512]{1,0:T(1,128)} %get-tuple-element.9.best_in, f32[16,768]{1,0:T(8,128)} %get-tuple-element.10.sums_in, f32[8,128]{1,0:T(8,128)} %get-tuple-element.11.counts_in), custom_call_target="tpu_custom_call" | custom-call | tf_op jit(solution)/shard_map/pallas_call | solution.py:476

commit v5 on v4

--- a/solution.py
+++ b/solution.py
@@ -276,13 +276,6 @@
                 mixed = jnp.where(lane == CL_DEV + g, tally[pl.ds(16 * q + 8 * g, 8), :], mixed)
             late[q, :, pl.ds(D, 128)] = mixed.astype(jnp.bfloat16)
 
-    for j in range(2, 6):
-        loads[1 + j].wait()
-        at, n = index_parts[j]
-        step = CH if n % CH == 0 else UC
-        for k in range(n // step):
-            normalize(ir, pl.multiple_of(at + step * k, 16), step)
-
     pl.semaphore_wait(barrier, len(partners))
     for cp in code:
         cp.start()
@@ -292,6 +285,13 @@
     for cp in cr + ac:
         cp.start()
     to_sib[0].start()
+    for j in range(2, 6):
+        loads[1 + j].wait()
+        at, n = index_parts[j]
+        step = CH if n % CH == 0 else UC
+        for k in range(n // step):
+            normalize(ir, pl.multiple_of(at + step * k, 16), step)
+
     own_range(0, ROWS)
     count, _ = weigh(0, 0, 0)
     tally[...] = jnp.broadcast_to(count, (PLANE, 128))

time: 57.9 us -> 57.7 us (level)
  no operation moved by 1% of the time
where the time goes in v5:
time: 57.7 us; the launch traced here: 57.4 us
  Pallas kernels  56.8 us (98%)
  between operations  0.64 us (1%)
    pallas_call x1, Pallas kernels, per_device(): pl.pallas_call(window_kernel, out_shape=(jax.ShapeDtypeStruct((1, ROWS),...  55.4 us
    pallas_call x1, Pallas kernels, per_device(): pl.pallas_call(parted, out_shape=(jax.ShapeDtypeStruct((1, ROWS), f32), j...  1.43 us

profile of v5, /device:TPU:1, one launch (start us, length us, event | category | flops | bytes accessed | tf_op | source)
XLA Modules:
  0.0 57.4 jit_solution(8245924778447117066)
XLA Ops:
  0.6 55.4 %shard_map.85 = (f32[1,512]{1,0:T(1,128)}, f32[16,768]{1,0:T(8,128)}, f32[8,128]{1,0:T(8,128)}) custom-call(bf16[512,768]{1,0:T(8,128)(2,1)} %new_hbm.1, bf16[4096,768]{1,0:T(8,128)(2,1)} %index_hbm.1, s32[8,128]{1,0:T(8,128)} %bitcast.6, s32[1,256]{1,0:T(1,128)} %bitcast.8, s32[1,256]{1,0:T(1,128)} %bitcast.9, s32[1,256]{1,0:T(1,128)} %bitcast.10), custom_call_target="tpu_custom_call" | custom-call | flops 25769803776 | bytes 10485760 | tf_op jit(solution)/shard_map/pallas_call | solution.py:430
  56.0 1.4 %shard_map.86 = (f32[1,512]{1,0:T(1,128)}, f32[16,768]{1,0:T(8,128)}, f32[1,16]{1,0:T(1,128)}) custom-call(f32[1,512]{1,0:T(1,128)} %get-tuple-element.9.best_in, f32[16,768]{1,0:T(8,128)} %get-tuple-element.10.sums_in, f32[8,128]{1,0:T(8,128)} %get-tuple-element.11.counts_in), custom_call_target="tpu_custom_call" | custom-call | tf_op jit(solution)/shard_map/pallas_call | solution.py:476
